TPU v7x, 32 devices: a whole 2x2x4 slice. The times are simulated.
32 devices in a mesh: ctx: 8 (over y, x, core), fsdp: 4 (over z).
Axes of the slice: x: 2, y: 2, z: 4, core: 2. Of those that a mesh axis runs over, the one named last changes fastest.
Arguments:
- inner: bfloat16 [16384, 8192], P('ctx', 'fsdp'), may hold values from -6 to 6
- proj_weight: bfloat16 [32, 8192], P(None, 'fsdp'), may hold values from -0.0625 to 0.0625
- rates: float32 [8192], P('fsdp'), may hold values from 3.0517578e-06 to 0.0333333333
- keep: float32 [16384], P('ctx'), may hold values from 0.216 to 1, as said below
- skip: float32 [8192], P('fsdp'), may hold values from 0.5 to 1.5
- upstream: bfloat16 [16384, 8192], P('ctx', 'fsdp'), may hold values from -6 to 6
Outputs:
- input_grad: bfloat16 [16384, 8192], P('ctx', 'fsdp')
- proj_grad: float32 [32, 8192], P(None, 'fsdp')
Inputs may be any that keep to these rules, and one draw needn't show every extreme that they name: `keep`: factors on the tokens' decays.
All inputs are finite; a program needn't handle non-finite values.
Results may differ from a plain program's by a relative error of at most 0.0058.
Values sent between devices are 32-bit elements; how exact they have to be, the bound alone decides.
A program may use at most 128 MiB of HBM per device.

v0:
```python
import jax
import jax.numpy as jnp
from jax import lax
from jax.sharding import PartitionSpec as P

BLK = 256


def carried_in(shard, axis, combine, identity, reverse):
    length, place = (lax.axis_size(axis), lax.axis_index(axis))
    everything = jax.tree.map(lambda part: lax.all_gather(part, axis), shard)
    start = jax.tree.map(
        lambda part, zero: jnp.broadcast_to(jnp.asarray(zero, part.dtype), part.shape),
        shard,
        identity,
    )

    def step(k, before):
        at = length - 1 - k if reverse else k
        reached = at > place if reverse else at < place
        new = combine(before, jax.tree.map(lambda part: part[at], everything))
        return jax.tree.map(lambda a, b: jnp.where(reached, a, b), new, before)

    return lax.fori_loop(0, length, step, start)


def batched(form, left, right):
    return jnp.einsum(form, left, right, preferred_element_type=jnp.float32)


def precise(form, left, right):
    return jnp.einsum(
        form, left, right, precision=lax.Precision.HIGHEST, preferred_element_type=jnp.float32
    )


def combine(earlier, later):
    return (earlier[0] * later[0], later[1] + later[0][None, :] * earlier[1])


def local(inner, proj_weight, rates, keep, skip, upstream):
    length = inner.shape[0]
    channels = inner.shape[1]
    nstate = proj_weight.shape[0] // 2
    nblocks = length // BLK
    partial_coef = lax.dot_general(
        inner, proj_weight, (((1,), (1,)), ((), ())), preferred_element_type=jnp.float32
    )
    coeffs = lax.psum(partial_coef, "fsdp")
    coef_wide = coeffs.reshape(nblocks, BLK, 2 * nstate)
    write_wide = coef_wide[:, :, :nstate]
    read_wide = coef_wide[:, :, nstate:]
    coef_blocks = coeffs.astype(jnp.bfloat16).reshape(nblocks, BLK, 2 * nstate)
    write_coef = coef_blocks[:, :, :nstate]
    read_coef = coef_blocks[:, :, nstate:]
    factor = 1.0 / jnp.sqrt(jnp.float32(nstate))
    input_scale = jnp.sqrt(-jnp.expm1(-2.0 * rates))
    offsets = jnp.arange(1, BLK + 1).astype(jnp.float32)
    within_base = jnp.exp(-offsets[:, None] * rates[None, :])
    within = within_base[None] * jnp.cumprod(keep.reshape(nblocks, BLK), axis=1)[:, :, None]
    upstream_f = upstream.astype(jnp.float32).reshape(nblocks, BLK, channels)
    scaled = (
        input_scale[None, None, :]
        * inner.astype(jnp.float32).reshape(nblocks, BLK, channels)
        / within
    ).astype(jnp.bfloat16)
    weighted = (within * upstream_f).astype(jnp.bfloat16)
    decays = within[:, -1]
    state_terms = decays[:, None, :] * batched("jbn,jbe->jne", write_coef, scaled)
    adjoint_terms = factor * batched("jbn,jbe->jne", read_coef, weighted)

    def forward(state, item):
        return (item[0][None, :] * state + item[1], state)

    def backward(adjoint, item):
        return (item[1] + item[0][None, :] * adjoint, adjoint)

    zero_state = jnp.zeros((nstate, channels), jnp.float32)
    state_end, state_local = lax.scan(forward, zero_state, (decays, state_terms))
    adjoint_start, adjoint_local = lax.scan(
        backward, zero_state, (decays, adjoint_terms), reverse=True
    )
    device_decay = jnp.prod(decays, axis=0)
    ones_row = jnp.ones((1, channels), jnp.float32)
    before = jnp.concatenate([ones_row, jnp.cumprod(decays, axis=0)[:-1]], axis=0)
    after = jnp.flip(
        jnp.concatenate([ones_row, jnp.cumprod(jnp.flip(decays, 0), axis=0)[:-1]], axis=0), 0
    )
    identity = (jnp.ones_like(device_decay), zero_state)
    _, state_in = carried_in((device_decay, state_end), "ctx", combine, identity, False)
    _, adjoint_in = carried_in((device_decay, adjoint_start), "ctx", combine, identity, True)
    state_at = (state_local + before[:, None, :] * state_in[None]).astype(jnp.bfloat16)
    adjoint_at = adjoint_local + after[:, None, :] * adjoint_in[None]
    carried = (decays[:, None, :] * adjoint_at).astype(jnp.bfloat16)
    lower_mask = jnp.tril(jnp.ones((BLK, BLK), dtype=bool))
    read_write = jnp.where(
        lower_mask[None], batched("jbn,jcn->jbc", read_coef, write_coef), 0.0
    ).astype(jnp.bfloat16)
    grad_cross = jnp.where(lower_mask[None], batched("jbe,jce->jbc", weighted, scaled), 0.0)
    scan_grad = (
        input_scale[None, None, :]
        / within
        * (
            factor * batched("jbc,jbe->jce", read_write, weighted)
            + batched("jcn,jne->jce", write_coef, carried)
        )
    )
    grad_write = factor * precise("jbc,jbn->jcn", grad_cross, read_wide) + batched(
        "jce,jne->jcn", scaled, carried
    )
    grad_read = factor * (
        batched("jbe,jne->jbn", weighted, state_at)
        + precise("jbc,jcn->jbn", grad_cross, write_wide)
    )
    partial_grad = jnp.concatenate([grad_write, grad_read], axis=2).reshape(length, 2 * nstate)
    grad_coef = lax.psum(partial_grad, "fsdp")
    grad_short = grad_coef.astype(jnp.bfloat16)
    back_grad = jnp.dot(grad_short, proj_weight, preferred_element_type=jnp.float32)
    input_grad = (
        scan_grad.reshape(length, channels)
        + skip[None, :] * upstream_f.reshape(length, channels)
        + back_grad
    ).astype(jnp.bfloat16)
    local_proj = lax.dot_general(
        grad_coef,
        inner.astype(jnp.float32),
        (((0,), (0,)), ((), ())),
        precision=lax.Precision.HIGHEST,
        preferred_element_type=jnp.float32,
    )
    proj_total = lax.psum(local_proj, "ctx")
    return (input_grad, proj_total / (length * lax.axis_size("ctx")))


def solution(mesh):
    placed = (P("ctx", "fsdp"), P(None, "fsdp"), P("fsdp"), P("ctx"), P("fsdp"), P("ctx", "fsdp"))
    return jax.shard_map(
        local,
        mesh=mesh,
        in_specs=placed,
        out_specs=(P("ctx", "fsdp"), P(None, "fsdp")),
        check_vma=False,
    )
```

profile of v0, /device:TPU:0, one launch (start us, length us, event | category | flops | bytes accessed | tf_op | source)
XLA Modules:
  0.0 252.1 jit_solution(15752679022758044592)
XLA Ops:
  8.1 6.7 %fusion.49 = f32[2048,32]{0,1:T(8,128)} fusion(bf16[2048,2048]{1,0:T(8,128)(2,1)} %param.14, bf16[32,2048]{1,0:T(8,128)(2,1)S(1)} %copy-done), kind=kOutput, calls=%fused_computation.70 | convolution fusion | flops 268435456 | bytes 8781824 | tf_op jit(solution)/shard_map/dot_general | solution.py:46
  16.2 16.4 %fusion.4 = (bf16[8,256,2048]{2,1,0:T(8,128)(2,1)}, bf16[8,256,2048]{2,1,0:T(8,128)(2,1)S(1)}, f32[8,256,2048]{2,1,0:T(8,128)}) fusion(bf16[8,256,2048]{2,1,0:T(8,128)(2,1)} %bitcast.83, f32[8,256]{1,0:T(8,128)S(1)} %multiply_bitcast_fusion, f32[256,2048]{1,0:T(8,128)S(1)} %multiply_exponential_fusion, f32[2048]{0:T(1024)S(1)} %negate_sqrt_fusion, ...), kind=kLoop, calls=%fused_computation.17 | loop fusion | flops 33554432 | bytes 52445184 | tf_op jit(solution)/shard_map/convert_element_type | solution.py:66
  32.6 10.1 %fusion.50 = f32[8,256,256]{2,1,0:T(8,128)} fusion(bf16[8,256,2048]{2,1,0:T(8,128)(2,1)S(1)} %get-tuple-element.481, bf16[8,256,2048]{2,1,0:T(8,128)(2,1)} %get-tuple-element.480), kind=kOutput, calls=%fused_computation.71 | convolution fusion | flops 2147483648 | bytes 18874368 | tf_op jit(solution)/shard_map/jbe,jce->jbc/dot_general | solution.py:28
  42.7 1.1 slice_reduce_fusion.1
  44.2 10.7 %all-gather.1 = f32[16384]{0:T(1024)S(1)} all-gather(f32[2048]{0:T(1024)S(1)} %get-tuple-element.478), channel_id=3, replica_groups=mesh['ctx'=8,'fsdp'=4] {'ctx'}, dimensions={0}, use_global_device_ids=true | all-gather | bytes 73728 | tf_op jit(solution)/shard_map/all_gather | solution.py:11
  56.4 5.6 %convolution_multiply_fusion.1 = f32[8,16,2048]{2,1,0:T(8,128)} fusion(bf16[8,256,2048]{2,1,0:T(8,128)(2,1)} %copy-done.1, bf16[8,256,16]{1,0,2:T(8,128)(2,1)S(1)} %get-tuple-element.486), kind=kOutput, calls=%fused_computation.24 | convolution fusion | flops 134479872 | bytes 9502720 | tf_op jit(solution)/shard_map/jbn,jbe->jne/dot_general | solution.py:28
  62.0 8.3 %while.60 = (s32[]{:T(128)}, f32[16,2048]{1,0:T(8,128)S(1)}, f32[8,16,2048]{2,1,0:T(8,128)S(1)}, f32[8,16,2048]{2,1,0:T(8,128)}, f32[8,2048]{1,0:T(8,128)S(1)}, /*index=5*/s32[]{:T(128)}, s32[]{:T(128)}, s32[]{:T(128)}) while((s32[]{:T(128)}, f32[16,2048]{1,0:T(8,128)S(1)}, f32[8,16,2048]{2,1,0:T(8,128)S(1)}, ...), condition=%wide.region_4.5_spmd.clone, body=%wide.region_3.4_spmd.clone.sunk | while | flops 131076 | bytes 680056 | solution.py:80
  71.5 5.6 %convolution_multiply_fusion = f32[8,16,2048]{2,1,0:T(8,128)} fusion(bf16[8,256,2048]{2,1,0:T(8,128)(2,1)} %get-tuple-element.480, f32[8,2048]{1,0:T(8,128)S(1)} %get-tuple-element.713, bf16[8,256,16]{1,0,2:T(8,128)(2,1)S(1)} %get-tuple-element.485), kind=kOutput, calls=%fused_computation.23 | convolution fusion | flops 134479872 | bytes 9568256 | tf_op jit(solution)/shard_map/jbn,jbe->jne/dot_general | solution.py:28
  77.1 8.3 %while.62 = (s32[]{:T(128)}, f32[16,2048]{1,0:T(8,128)S(1)}, f32[8,16,2048]{2,1,0:T(8,128)S(1)}, f32[8,2048]{1,0:T(8,128)S(1)}, f32[8,16,2048]{2,1,0:T(8,128)}, /*index=5*/s32[]{:T(128)}, s32[]{:T(128)}) while((s32[]{:T(128)}, f32[16,2048]{1,0:T(8,128)S(1)}, f32[8,16,2048]{2,1,0:T(8,128)S(1)}, f32[8,2048]{1,0:T(8,128)S(1)}, ...), condition=%wide.region_10.11_spmd.clone, body=%wide.region_9.10_spmd.clone.sunk | while | flops 131075 | bytes 680036 | solution.py:79
  77.2 1.0 bitcast_add_fusion.8
  78.2 1.0 bitcast_add_fusion.8
  79.3 1.0 bitcast_add_fusion.8
  80.3 1.0 bitcast_add_fusion.8
  81.4 1.0 bitcast_add_fusion.8
  82.4 1.0 bitcast_add_fusion.8
  83.4 1.0 bitcast_add_fusion.8
  84.5 1.0 bitcast_add_fusion.8
  85.6 11.2 %fusion.11 = f32[8,256,2048]{2,1,0:T(8,128)} fusion(bf16[8,256,2048]{2,1,0:T(8,128)(2,1)} %copy-done.1, pred[256,256]{1,0:T(8,128)(4,1)S(1)} %iota_compare_fusion, bf16[8,256,16]{1,0,2:T(8,128)(2,1)S(1)} %get-tuple-element.486, bf16[8,256,16]{1,0,2:T(8,128)(2,1)S(1)} %get-tuple-element.485), kind=kOutput, calls=%fused_computation.31 | convolution fusion | flops 2165309440 | bytes 25362432 | tf_op jit(solution)/shard_map/jbc,jbe->jce/dot_general | solution.py:28
  96.9 8.2 %while.61 = (s32[]{:T(128)}, f32[16,2048]{1,0:T(8,128)S(1)}, s32[]{:T(128)}, f32[8,16,2048]{2,1,0:T(8,128)}, f32[8,2048]{1,0:T(8,128)S(1)}, /*index=5*/s32[]{:T(128)}, s32[]{:T(128)}, s32[]{:T(128)}, s32[]{:T(128)}) while((s32[]{:T(128)}, f32[16,2048]{1,0:T(8,128)S(1)}, s32[]{:T(128)}, f32[8,16,2048]{2,1,0:T(8,128)}, ...), condition=%wide.region_8.9_spmd.clone, body=%wide.region_7.8_spmd.clone.sunk | while | flops 131080 | bytes 417959 | solution.py:24
  103.1 1.0 fusion.66
  105.1 15.6 %all-gather.8.cloned.1.call-done = f32[128,2048]{1,0:T(8,128)} async-done(((f32[16,2048]{1,0:T(8,128)}), f32[128,2048]{1,0:T(8,128)}) %all-gather.8.cloned.1.call-update) | async-done | bytes 1048592 | tf_op jit(solution)/shard_map/all_gather | solution.py:11
  120.7 8.1 %while.63 = (s32[]{:T(128)}, f32[16,2048]{1,0:T(8,128)S(1)}, s32[]{:T(128)}, f32[8,16,2048]{2,1,0:T(8,128)}, f32[8,2048]{1,0:T(8,128)S(1)}, /*index=5*/s32[]{:T(128)}, s32[]{:T(128)}) while((s32[]{:T(128)}, f32[16,2048]{1,0:T(8,128)S(1)}, s32[]{:T(128)}, f32[8,16,2048]{2,1,0:T(8,128)}, f32[8,2048]{1,0:T(8,128)S(1)}, ...), condition=%wide.region_13.14_spmd.clone, body=%wide.region_12.13_spmd.clone.sunk | while | flops 131076 | bytes 417897 | solution.py:24
  128.8 5.9 %fusion.46 = f32[8,256,16]{1,2,0:T(8,128)S(1)} fusion(bf16[8,256,2048]{2,1,0:T(8,128)(2,1)} %get-tuple-element.480, f32[8,16,2048]{2,1,0:T(8,128)} %copy-done.8, f32[16,2048]{1,0:T(8,128)S(1)} %get-tuple-element.362, f32[8,2048]{1,0:T(8,128)S(1)} %rev.8, f32[8,2048]{1,0:T(8,128)S(1)} %get-tuple-element.714), kind=kOutput, calls=%fused_computation.67 | convolution fusion | flops 135266304 | bytes 9830400 | tf_op jit(solution)/shard_map/jce,jne->jcn/dot_general | solution.py:28
  134.7 3.1 %fusion.15 = f32[8,256,16]{1,2,0:T(8,128)S(1)} fusion(f32[8,256,16]{1,2,0:T(8,128)S(1)} %fusion.46, f32[8,256,256]{2,1,0:T(8,128)} %fusion.50, pred[256,256]{1,0:T(8,128)(4,1)S(1)} %iota_compare_fusion, f32[8,256,16]{1,0,2:T(8,128)S(1)} %get-tuple-element.483), kind=kOutput, calls=%fused_computation.33 | convolution fusion | flops 101253120 | bytes 2555904 | tf_op jit(solution)/shard_map/jbc,jbn->jcn/dot_general | solution.py:32
  137.8 5.9 %fusion.30 = f32[8,256,16]{1,2,0:T(8,128)S(1)} fusion(bf16[8,256,2048]{2,1,0:T(8,128)(2,1)} %copy-done.1, f32[8,16,2048]{2,1,0:T(8,128)} %copy-done.7, f32[16,2048]{1,0:T(8,128)S(1)} %get-tuple-element.365, f32[8,2048]{1,0:T(8,128)S(1)} %concatenate.10), kind=kOutput, calls=%fused_computation.44 | convolution fusion | flops 135004160 | bytes 9764864 | tf_op jit(solution)/shard_map/jbe,jne->jbn/dot_general | solution.py:28
  143.7 2.0 fusion.21
  146.8 12.0 %fusion.2 = f32[8,256,2048]{2,1,0:T(8,128)} fusion(f32[8,256,2048]{2,1,0:T(8,128)} %fusion.11, f32[8,256]{1,0:T(8,128)S(1)} %multiply_bitcast_fusion, f32[256,2048]{1,0:T(8,128)S(1)} %copy-done.5, f32[2048]{0:T(1024)S(1)} %negate_sqrt_fusion, bf16[8,256,16]{1,0,2:T(8,128)(2,1)S(1)} %get-tuple-element.485, f32[8,16,2048]{2,1,0:T(8,128)} %copy-done.8, ...), kind=kOutput, calls=%fused_computation.15 | convolution fusion | flops 156237824 | bytes 37044224 | tf_op jit(solution)/shard_map/jcn,jne->jce/dot_general | solution.py:28
  158.8 23.2 %all-reduce.8.cloned.1.call-done = f32[2048,32]{0,1:T(8,128)} async-done(((f32[2048,32]{0,1:T(8,128)}), f32[2048,32]{0,1:T(8,128)}) %all-reduce.8.cloned.1.call-update) | async-done | bytes 262160 | tf_op jit(solution)/shard_map/psum | solution.py:116
  182.0 8.4 %fusion.51 = f32[32,2048]{1,0:T(8,128)} fusion(f32[2048,32]{0,1:T(8,128)} %all-reduce.8.cloned.1.call-done, bf16[2048,2048]{1,0:T(8,128)(2,1)} %param.14), kind=kOutput, calls=%fused_computation.72 | convolution fusion | flops 1610612736 | bytes 8912896 | tf_op jit(solution)/shard_map/dot_general | solution.py:124
  190.5 13.2 %fusion.6 = bf16[2048,2048]{1,0:T(8,128)(2,1)} fusion(f32[8,256,2048]{2,1,0:T(8,128)} %fusion.2, bf16[32,2048]{1,0:T(8,128)(2,1)S(1)} %copy-done, f32[2048]{0:T(1024)S(1)} %copy-done.12, bf16[2048,2048]{1,0:T(8,128)(2,1)} %param.19, f32[2048,32]{0,1:T(8,128)S(1)} %copy-done.9), kind=kOutput, calls=%fused_computation.21 | convolution fusion | flops 289472512 | bytes 33955840 | tf_op jit(solution)/shard_map/dot_general | solution.py:118
  203.6 40.3 %all-reduce.10.cloned.1.call-done = f32[32,2048]{1,0:T(8,128)} async-done(((f32[32,2048]{1,0:T(8,128)}), f32[32,2048]{1,0:T(8,128)}) %all-reduce.10.cloned.1.call-update) | async-done | bytes 262160 | tf_op jit(solution)/shard_map/psum | solution.py:131
  243.9 1.7 broadcast_multiply_fusion.1
  (142 shorter events, 29.5 us)
Async XLA Ops:
  7.2 0.9 copy-start
  7.2 7.7 %copy-start.13 = (f32[2048]{0:T(1024)S(1)}, f32[2048]{0:T(1024)}, u32[]{:S(2)}) copy-start(f32[2048]{0:T(1024)} %param.17) | copy-start | bytes 24580
  7.2 8.6 %copy-start.11 = (f32[2048]{0:T(1024)S(1)}, f32[2048]{0:T(1024)}, u32[]{:S(2)}) copy-start(f32[2048]{0:T(1024)} %param.16) | copy-start | bytes 24580
  7.2 48.1 %all-reduce.6.cloned.1.call-start = ((), (), s32[]{:S(2)}) async-start(), calls=%async_computation | async-start | bytes 524288 | tf_op jit(solution)/shard_map/psum | solution.py:49
  14.8 82.1 %all-gather.6.cloned.1.call-start = ((), (), s32[]{:S(2)}) async-start(), calls=%async_computation.3 | async-start | bytes 1179648 | tf_op jit(solution)/shard_map/all_gather | solution.py:11
  16.1 16.4 %copy-start.4 = (f32[256,2048]{1,0:T(8,128)}, f32[256,2048]{1,0:T(8,128)S(1)}, u32[]{:S(2)}) copy-start(f32[256,2048]{1,0:T(8,128)S(1)} %multiply_exponential_fusion) | copy-start | bytes 6291460
  32.5 10.1 %copy-start.1 = (bf16[8,256,2048]{2,1,0:T(8,128)(2,1)}, bf16[8,256,2048]{2,1,0:T(8,128)(2,1)S(1)}, u32[]{:S(2)}) copy-start(bf16[8,256,2048]{2,1,0:T(8,128)(2,1)S(1)} %get-tuple-element.481) | copy-start | bytes 25165828
  70.4 0.7 copy-start.3
  70.4 1.1 copy-start.8
  71.0 14.4 %copy-start.10 = (f32[2048,32]{0,1:T(8,128)S(1)}, f32[2048,32]{0,1:T(8,128)}, u32[]{:S(2)}) copy-start(f32[2048,32]{0,1:T(8,128)} %all-reduce.6.cloned.1.call-done) | copy-start | bytes 786436
  71.1 49.7 %all-gather.8.cloned.1.call-start = ((), (), s32[]{:S(2)}) async-start(), calls=%async_computation.4 | async-start | bytes 1179648 | tf_op jit(solution)/shard_map/all_gather | solution.py:11
  85.5 11.3 %copy-start.2 = (f32[16,2048]{1,0:T(8,128)}, f32[16,2048]{1,0:T(8,128)S(1)}, u32[]{:S(2)}) copy-start(f32[16,2048]{1,0:T(8,128)S(1)} %get-tuple-element.364) | copy-start | bytes 393220
  85.5 11.3 %copy-start.7 = (f32[8,16,2048]{2,1,0:T(8,128)}, f32[8,16,2048]{2,1,0:T(8,128)S(1)}, u32[]{:S(2)}) copy-start(f32[8,16,2048]{2,1,0:T(8,128)S(1)} %get-tuple-element.363) | copy-start | bytes 3145732
  96.8 85.2 %all-reduce.8.cloned.1.call-start = ((), (), s32[]{:S(2)}) async-start(), calls=%async_computation.1 | async-start | bytes 524288 | tf_op jit(solution)/shard_map/psum | solution.py:116
  134.7 9.0 %copy-start.6 = (f32[8,256,256]{2,1,0:T(8,128)S(1)}, f32[8,256,256]{2,1,0:T(8,128)}, u32[]{:S(2)}) copy-start(f32[8,256,256]{2,1,0:T(8,128)} %fusion.50) | copy-start | bytes 6291460
  134.7 12.1 %copy-start.5 = (f32[256,2048]{1,0:T(8,128)S(1)}, f32[256,2048]{1,0:T(8,128)}, u32[]{:S(2)}) copy-start(f32[256,2048]{1,0:T(8,128)} %copy-done.4) | copy-start | bytes 6291460
  146.5 97.3 %all-reduce.10.cloned.1.call-start = ((), (), s32[]{:S(2)}) async-start(), calls=%async_computation.2 | async-start | bytes 524288 | tf_op jit(solution)/shard_map/psum | solution.py:131
  158.8 31.7 %copy-start.12 = (f32[2048]{0:T(1024)S(1)}, f32[2048]{0:T(1024)}, u32[]{:S(2)}) copy-start(f32[2048]{0:T(1024)} %param.18) | copy-start | bytes 24580
  182.0 8.5 %copy-start.9 = (f32[2048,32]{0,1:T(8,128)S(1)}, f32[2048,32]{0,1:T(8,128)}, u32[]{:S(2)}) copy-start(f32[2048,32]{0,1:T(8,128)} %all-reduce.8.cloned.1.call-done) | copy-start | bytes 786436
Sparse Core Ops, SparseCore 0:
  14.9 37.9 all-reduce.5
  71.2 23.7 all-gather.5
  97.0 23.6 all-gather.7
  146.7 35.2 all-reduce.7
  190.6 53.2 all-reduce.9
where the time goes:
time: 253 us; the launch traced here: 252 us
  matrix products  89.6 us (35%)
  waiting for transfers between devices  79.2 us (31%)
  other arithmetic  52.9 us (21%)
  between operations  14.1 us (6%)
  blocking collectives  10.7 us (4%)
  local copies, waits for them, and re-layouts  3.93 us (2%)
    dot_general x7, matrix products, batched(): return jnp.einsum(form, left, right, preferred_element_type=jnp.float32)  56.2 us
    psum x1, waiting for transfers between devices, local(): proj_total = lax.psum(local_proj, 'ctx')  40.3 us
    psum x1, waiting for transfers between devices, local(): grad_coef = lax.psum(partial_grad, 'fsdp')  23.2 us
    convert_element_type x1, other arithmetic, local(): scaled = (input_scale[None, None, :] * inner.astype(jnp.float32).reshape(...  16.4 us
    all_gather x2, waiting for transfers between devices, carried_in(): everything = jax.tree.map(lambda part: lax.all_gather(part, axis), shard)  15.6 us
    select_n x16, other arithmetic, step(): return jax.tree.map(lambda a, b: jnp.where(reached, a, b), new, before)  15.6 us
    dot_general x1, matrix products, local(): jnp.dot(grad_short, proj_weight, preferred_element_type=jnp.float32)  13.2 us
    all_gather x1, blocking collectives, carried_in(): everything = jax.tree.map(lambda part: lax.all_gather(part, axis), shard)  10.7 us
  transfers between devices with their start and end apart: 5, of which 3 were waited for; matrix products, arithmetic and copies ran while one was open for 35% of the time, Pallas kernels for 0%

commit v1 on v0

--- a/solution.py
+++ b/solution.py
@@ -1,27 +1,135 @@
+import functools
+
 import jax
 import jax.numpy as jnp
 from jax import lax
+from jax.experimental import pallas as pl
+from jax.experimental.pallas import tpu as pltpu
 from jax.sharding import PartitionSpec as P
 
 BLK = 256
-
-
-def carried_in(shard, axis, combine, identity, reverse):
-    length, place = (lax.axis_size(axis), lax.axis_index(axis))
-    everything = jax.tree.map(lambda part: lax.all_gather(part, axis), shard)
-    start = jax.tree.map(
-        lambda part, zero: jnp.broadcast_to(jnp.asarray(zero, part.dtype), part.shape),
-        shard,
-        identity,
-    )
-
-    def step(k, before):
-        at = length - 1 - k if reverse else k
-        reached = at > place if reverse else at < place
-        new = combine(before, jax.tree.map(lambda part: part[at], everything))
-        return jax.tree.map(lambda a, b: jnp.where(reached, a, b), new, before)
-
-    return lax.fori_loop(0, length, step, start)
+MESH = pl.DeviceIdType.MESH
+
+
+def greet(axis, n):
+    me = lax.axis_index(axis)
+    barrier = pltpu.get_barrier_semaphore()
+    for k in range(1, n):
+        pl.semaphore_signal(
+            barrier, inc=1, device_id={axis: lax.rem(me + k, n)}, device_id_type=MESH
+        )
+    pl.semaphore_wait(barrier, n - 1)
+    return me
+
+
+def send(axis, n, me, k, src, dst, sems):
+    copy = pltpu.make_async_remote_copy(
+        src_ref=src,
+        dst_ref=dst,
+        send_sem=sems[0].at[k - 1],
+        recv_sem=sems[1].at[k - 1],
+        device_id={axis: lax.rem(me + k, n)},
+        device_id_type=MESH,
+    )
+    copy.start()
+    return copy
+
+
+def reduce_kernel(axis, n, x_ref, o_ref, parts, total, s1, r1, s2, r2):
+    me = greet(axis, n)
+    copies = [
+        send(axis, n, me, k, x_ref.at[lax.rem(me + k, n)], parts.at[k - 1], (s1, r1))
+        for k in range(1, n)
+    ]
+    acc = x_ref[me]
+    for k in range(1, n):
+        copies[k - 1].wait_recv()
+        acc = acc + parts[k - 1]
+    total[me] = acc
+    back = [send(axis, n, me, k, total.at[me], total.at[me], (s2, r2)) for k in range(1, n)]
+    for copy in copies:
+        copy.wait_send()
+    for copy in back:
+        copy.wait()
+    o_ref[...] = total[...]
+
+
+def reduced(x, axis, ident):
+    n = x.shape[0]
+    vmem = pl.BlockSpec(memory_space=pltpu.VMEM)
+    return pl.pallas_call(
+        functools.partial(reduce_kernel, axis, n),
+        out_shape=jax.ShapeDtypeStruct(x.shape, x.dtype),
+        in_specs=[vmem],
+        out_specs=vmem,
+        scratch_shapes=[
+            pltpu.VMEM((n - 1,) + x.shape[1:], x.dtype),
+            pltpu.VMEM(x.shape, x.dtype),
+        ]
+        + [pltpu.SemaphoreType.DMA((n - 1,))] * 4,
+        compiler_params=pltpu.CompilerParams(collective_id=ident, has_side_effects=True),
+    )(x)
+
+
+def split(x, n):
+    rows, length = x.shape
+    return x.reshape(rows, n, length // n).transpose(1, 0, 2)
+
+
+def join(x):
+    n, rows, part = x.shape
+    return x.transpose(1, 0, 2).reshape(rows, n * part)
+
+
+def all_reduced(x, axis, ident):
+    return join(reduced(split(x, lax.axis_size(axis)), axis, ident))
+
+
+def scan_kernel(axis, n, nstate, x_ref, o_ref, got, out, home, s1, r1, s2, r2):
+    me = greet(axis, n)
+    copies = [
+        send(axis, n, me, k, x_ref.at[lax.rem(me + k, n)], got.at[me], (s1, r1))
+        for k in range(1, n)
+    ]
+    got[me] = x_ref[me]
+    for copy in copies:
+        copy.wait()
+    zero = jnp.zeros((nstate, x_ref.shape[2]), jnp.float32)
+    state = zero
+    adjoint = zero
+    for k in range(n):
+        out[k, :nstate] = state
+        state = got[k, :nstate] + got[k, 2 * nstate : 2 * nstate + 1] * state
+        j = n - 1 - k
+        out[j, nstate:] = adjoint
+        adjoint = got[j, nstate : 2 * nstate] + got[j, 2 * nstate : 2 * nstate + 1] * adjoint
+    back = [
+        send(axis, n, me, k, out.at[lax.rem(me + k, n)], home.at[me], (s2, r2))
+        for k in range(1, n)
+    ]
+    home[me] = out[me]
+    for copy in back:
+        copy.wait()
+    o_ref[...] = home[...]
+
+
+def scanned(x, nstate, axis, ident):
+    n, rows, part = x.shape
+    vmem = pl.BlockSpec(memory_space=pltpu.VMEM)
+    small = (n, 2 * nstate, part)
+    return pl.pallas_call(
+        functools.partial(scan_kernel, axis, n, nstate),
+        out_shape=jax.ShapeDtypeStruct(small, x.dtype),
+        in_specs=[vmem],
+        out_specs=vmem,
+        scratch_shapes=[
+            pltpu.VMEM(x.shape, x.dtype),
+            pltpu.VMEM(small, x.dtype),
+            pltpu.VMEM(small, x.dtype),
+        ]
+        + [pltpu.SemaphoreType.DMA((n - 1,))] * 4,
+        compiler_params=pltpu.CompilerParams(collective_id=ident, has_side_effects=True),
+    )(x)
 
 
 def batched(form, left, right):
@@ -32,10 +140,6 @@
     return jnp.einsum(
         form, left, right, precision=lax.Precision.HIGHEST, preferred_element_type=jnp.float32
     )
-
-
-def combine(earlier, later):
-    return (earlier[0] * later[0], later[1] + later[0][None, :] * earlier[1])
 
 
 def local(inner, proj_weight, rates, keep, skip, upstream):
@@ -44,9 +148,9 @@
     nstate = proj_weight.shape[0] // 2
     nblocks = length // BLK
     partial_coef = lax.dot_general(
-        inner, proj_weight, (((1,), (1,)), ((), ())), preferred_element_type=jnp.float32
-    )
-    coeffs = lax.psum(partial_coef, "fsdp")
+        proj_weight, inner, (((1,), (1,)), ((), ())), preferred_element_type=jnp.float32
+    )
+    coeffs = all_reduced(partial_coef, "fsdp", 0).T
     coef_wide = coeffs.reshape(nblocks, BLK, 2 * nstate)
     write_wide = coef_wide[:, :, :nstate]
     read_wide = coef_wide[:, :, nstate:]
@@ -86,9 +190,12 @@
     after = jnp.flip(
         jnp.concatenate([ones_row, jnp.cumprod(jnp.flip(decays, 0), axis=0)[:-1]], axis=0), 0
     )
-    identity = (jnp.ones_like(device_decay), zero_state)
-    _, state_in = carried_in((device_decay, state_end), "ctx", combine, identity, False)
-    _, adjoint_in = carried_in((device_decay, adjoint_start), "ctx", combine, identity, True)
+    packed = jnp.concatenate(
+        [state_end, adjoint_start, jnp.broadcast_to(device_decay[None, :], (8, channels))], axis=0
+    )
+    arrived = join(scanned(split(packed, lax.axis_size("ctx")), nstate, "ctx", 1))
+    state_in = arrived[:nstate]
+    adjoint_in = arrived[nstate:]
     state_at = (state_local + before[:, None, :] * state_in[None]).astype(jnp.bfloat16)
     adjoint_at = adjoint_local + after[:, None, :] * adjoint_in[None]
     carried = (decays[:, None, :] * adjoint_at).astype(jnp.bfloat16)
@@ -113,7 +220,7 @@
         + precise("jbc,jcn->jbn", grad_cross, write_wide)
     )
     partial_grad = jnp.concatenate([grad_write, grad_read], axis=2).reshape(length, 2 * nstate)
-    grad_coef = lax.psum(partial_grad, "fsdp")
+    grad_coef = all_reduced(partial_grad.T, "fsdp", 2).T
     grad_short = grad_coef.astype(jnp.bfloat16)
     back_grad = jnp.dot(grad_short, proj_weight, preferred_element_type=jnp.float32)
     input_grad = (
@@ -128,7 +235,7 @@
         precision=lax.Precision.HIGHEST,
         preferred_element_type=jnp.float32,
     )
-    proj_total = lax.psum(local_proj, "ctx")
+    proj_total = all_reduced(local_proj, "ctx", 3)
     return (input_grad, proj_total / (length * lax.axis_size("ctx")))
 
 

time: 253 us -> 218 us (0.86)
  waiting for transfers between devices: 79.2 us -> 0 us
  Pallas kernels: 0 us -> 64 us
  local copies, waits for them, and re-layouts: 3.93 us -> 24 us
  between operations: 14.1 us -> 0.94 us
  blocking collectives: 10.7 us -> 0 us
  other arithmetic: 52.9 us -> 44.8 us
  matrix products: 89.6 us -> 83.1 us
    pallas_call x0 -> x4, Pallas kernels: none -> 64 us  [the longest x3 49.9 us: reduced(): pl.pallas_call(functools.partial(reduce_kernel, axis, n), out_shape=jax.S...]
    psum x3 -> x0, waiting for transfers between devices: 63.5 us -> none  [the longest x1 40.3 us: local(): proj_total = lax.psum(local_proj, 'ctx')]
    all_gather x2 -> x0, waiting for transfers between devices: 15.6 us -> none  [carried_in(): everything = jax.tree.map(lambda part: lax.all_gather(part, axis), shard)]
    select_n x16 -> x0, other arithmetic: 15.6 us -> none  [step(): return jax.tree.map(lambda a, b: jnp.where(reached, a, b), new, before)]
    dot_general x0 -> x1, local copies, waits for them, and re-layouts: none -> 12.2 us  [local(): lax.dot_general(grad_coef, inner.astype(jnp.float32), (((0,), (0,)), ((),...]
    all_gather x1 -> x0, blocking collectives: 10.7 us -> none  [carried_in(): everything = jax.tree.map(lambda part: lax.all_gather(part, axis), shard)]
    dynamic_update_slice x16, other arithmetic: 0.22 us -> 10.6 us  [local(): lax.scan(forward, zero_state, (decays, state_terms))]
    dot_general x1, matrix products: 6.68 us -> 2.58 us  [local(): lax.dot_general(proj_weight, inner, (((1,), (1,)), ((), ())), preferred_e...]
  transfers between devices with their start and end apart: 5 -> 0, of which waited for: 3 -> 0; matrix products, arithmetic and copies ran while one was open for 35% -> 0% of each run, Pallas kernels for 0% -> 0%
where the time goes in v1:
time: 218 us; the launch traced here: 217 us
  matrix products  83.1 us (38%)
  Pallas kernels  64 us (29%)
  other arithmetic  44.8 us (21%)
  local copies, waits for them, and re-layouts  24 us (11%)
    dot_general x7, matrix products, batched(): return jnp.einsum(form, left, right, preferred_element_type=jnp.float32)  53.7 us
    pallas_call x3, Pallas kernels, reduced(): pl.pallas_call(functools.partial(reduce_kernel, axis, n), out_shape=jax.S...  49.9 us
    convert_element_type x1, other arithmetic, local(): scaled = (input_scale[None, None, :] * inner.astype(jnp.float32).reshape(...  14.6 us
    pallas_call x1, Pallas kernels, scanned(): pl.pallas_call(functools.partial(scan_kernel, axis, n, nstate), out_shape...  14.1 us
    dot_general x1, matrix products, local(): jnp.dot(grad_short, proj_weight, preferred_element_type=jnp.float32)  13.1 us
    dot_general x1, local copies, waits for them, and re-layouts, local(): lax.dot_general(grad_coef, inner.astype(jnp.float32), (((0,), (0,)), ((),...  12.2 us
    dynamic_update_slice x16, other arithmetic, local(): lax.scan(forward, zero_state, (decays, state_terms))  10.6 us
    dot_general x1, matrix products, local(): lax.dot_general(grad_coef, inner.astype(jnp.float32), (((0,), (0,)), ((),...  10.3 us

profile of v1, /device:TPU:0, one launch (start us, length us, event | category | flops | bytes accessed | tf_op | source)
XLA Modules:
  0.0 217.1 jit_solution(2489396811620546578)
XLA Ops:
  2.2 1.2 multiply_exponential_fusion
  4.2 14.6 %fusion.2 = (bf16[8,256,2048]{2,1,0:T(8,128)(2,1)}, bf16[8,256,2048]{2,1,0:T(8,128)(2,1)}, f32[8,256,2048]{2,1,0:T(8,128)S(1)}) fusion(bf16[8,256,2048]{2,1,0:T(8,128)(2,1)} %bitcast.111, f32[8,256]{1,0:T(8,128)S(1)} %multiply_bitcast_fusion.1, f32[256,2048]{1,0:T(8,128)S(1)} %multiply_exponential_fusion, f32[2048]{0:T(1024)S(1)} %negate_sqrt_fusion, ...), kind=kLoop, calls=%fused_computation.11 | loop fusion | flops 33554432 | bytes 52445184 | tf_op jit(solution)/shard_map/convert_element_type | solution.py:170
  19.0 2.6 %fusion.47 = f32[32,2048]{1,0:T(8,128)S(1)} fusion(bf16[32,2048]{1,0:T(8,128)(2,1)S(1)} %copy-done, bf16[2048,2048]{1,0:T(8,128)(2,1)S(1)} %bitcast.114), kind=kOutput, calls=%fused_computation.72 | convolution fusion | flops 268435456 | bytes 8781824 | tf_op jit(solution)/shard_map/dot_general | solution.py:150
  22.3 18.2 %shard_map.77 = f32[4,32,512]{2,1,0:T(8,128)} custom-call(f32[4,32,512]{2,1,0:T(8,128)} %bitcast.128), custom_call_target="tpu_custom_call" | custom-call | tf_op jit(solution)/shard_map/pallas_call | solution.py:60
  41.6 5.6 %convolution_multiply_fusion = f32[8,16,2048]{2,1,0:T(8,128)} fusion(bf16[8,256,2048]{2,1,0:T(8,128)(2,1)} %get-tuple-element.196, f32[8,2048]{1,0:T(8,128)S(1)} %bitcast.117, bf16[8,256,16]{1,0,2:T(8,128)(2,1)S(1)} %get-tuple-element.203), kind=kOutput, calls=%fused_computation.17 | convolution fusion | flops 134479872 | bytes 9568256 | tf_op jit(solution)/shard_map/jbn,jbe->jne/dot_general | solution.py:136
  47.2 1.1 broadcast.49.clone.1
  48.3 13.3 %while.31 = (s32[]{:T(128)}, f32[16,2048]{1,0:T(8,128)S(1)}, f32[8,16,2048]{2,1,0:T(8,128)}, f32[8,2048]{1,0:T(8,128)S(1)}, f32[8,16,2048]{2,1,0:T(8,128)}, /*index=5*/s32[]{:T(128)}, s32[]{:T(128)}) while((s32[]{:T(128)}, f32[16,2048]{1,0:T(8,128)S(1)}, f32[8,16,2048]{2,1,0:T(8,128)}, f32[8,2048]{1,0:T(8,128)S(1)}, ...), condition=%wide.region_6.7_spmd.clone, body=%wide.region_5.6_spmd.clone.sunk | while | flops 131075 | bytes 680544 | solution.py:183
  49.0 1.0 bitcast_add_fusion.6
  50.7 1.0 bitcast_add_fusion.6
  52.3 1.0 bitcast_add_fusion.6
  55.7 1.0 bitcast_add_fusion.6
  57.4 1.0 bitcast_add_fusion.6
  59.0 1.0 bitcast_add_fusion.6
  61.7 5.6 %convolution_multiply_fusion.1 = f32[8,16,2048]{2,1,0:T(8,128)} fusion(bf16[8,256,2048]{2,1,0:T(8,128)(2,1)} %get-tuple-element.197, bf16[8,256,16]{1,0,2:T(8,128)(2,1)S(1)} %get-tuple-element.204), kind=kOutput, calls=%fused_computation.18 | convolution fusion | flops 134479872 | bytes 9502720 | tf_op jit(solution)/shard_map/jbn,jbe->jne/dot_general | solution.py:136
  67.3 1.2 broadcast.49.clone
  68.4 13.4 %while.30 = (s32[]{:T(128)}, f32[16,2048]{1,0:T(8,128)S(1)}, f32[8,16,2048]{2,1,0:T(8,128)}, f32[8,16,2048]{2,1,0:T(8,128)}, f32[8,2048]{1,0:T(8,128)S(1)}, /*index=5*/s32[]{:T(128)}, s32[]{:T(128)}, s32[]{:T(128)}) while((s32[]{:T(128)}, f32[16,2048]{1,0:T(8,128)S(1)}, f32[8,16,2048]{2,1,0:T(8,128)}, f32[8,16,2048]{2,1,0:T(8,128)}, ...), condition=%wide.region_3.4_spmd.clone, body=%wide.region_2.3_spmd.clone.sunk | while | flops 131076 | bytes 680056 | solution.py:184
  82.6 14.1 %shard_map.78 = f32[8,32,256]{2,1,0:T(8,128)} custom-call(f32[8,40,256]{2,1,0:T(8,128)} %bitcast.124), custom_call_target="tpu_custom_call" | custom-call | tf_op jit(solution)/shard_map/pallas_call | solution.py:120
  96.7 1.0 slice_bitcast_fusion
  98.6 5.9 %fusion.44 = f32[8,256,16]{1,2,0:T(8,128)S(1)} fusion(bf16[8,256,2048]{2,1,0:T(8,128)(2,1)} %get-tuple-element.196, f32[8,16,2048]{2,1,0:T(8,128)} %get-tuple-element.134, f32[16,2048]{1,0:T(8,128)S(1)} %bitcast.135, f32[8,2048]{1,0:T(8,128)S(1)} %rev.8, f32[8,2048]{1,0:T(8,128)S(1)} %get-tuple-element.313), kind=kOutput, calls=%fused_computation.69 | convolution fusion | flops 135266304 | bytes 9830400 | tf_op jit(solution)/shard_map/jce,jne->jcn/dot_general | solution.py:136
  104.4 8.1 %fusion.48 = f32[8,256,256]{2,1,0:T(8,128)S(1)} fusion(bf16[8,256,2048]{2,1,0:T(8,128)(2,1)} %get-tuple-element.197, bf16[8,256,2048]{2,1,0:T(8,128)(2,1)} %get-tuple-element.196), kind=kOutput, calls=%fused_computation.73 | convolution fusion | flops 2147483648 | bytes 18874368 | tf_op jit(solution)/shard_map/jbe,jce->jbc/dot_general | solution.py:136
  112.7 1.2 copy-done.1
  113.9 1.4 fusion.13
  115.4 6.0 %fusion.28 = f32[8,256,16]{1,2,0:T(8,128)S(1)} fusion(bf16[8,256,2048]{2,1,0:T(8,128)(2,1)} %get-tuple-element.197, f32[8,16,2048]{2,1,0:T(8,128)} %get-tuple-element.137, f32[16,2048]{1,0:T(8,128)S(1)} %bitcast.137, f32[8,2048]{1,0:T(8,128)S(1)} %concatenate.14), kind=kOutput, calls=%fused_computation.39 | convolution fusion | flops 135004160 | bytes 9764864 | tf_op jit(solution)/shard_map/jbe,jne->jbn/dot_general | solution.py:136
  121.4 2.0 fusion.19
  124.2 18.0 %shard_map.79 = f32[4,32,512]{2,1,0:T(8,128)} custom-call(f32[4,32,512]{2,1,0:T(8,128)} %bitcast.131), custom_call_target="tpu_custom_call" | custom-call | tf_op jit(solution)/shard_map/pallas_call | solution.py:60
  142.2 1.1 copy.23
  143.5 12.2 %copy.27 = bf16[2048,2048]{1,0:T(8,128)(2,1)} copy(bf16[2048,2048]{0,1:T(8,128)(2,1)} %bitcast.112) | data formatting | bytes 16777216 | tf_op jit(solution)/shard_map/dot_general | solution.py:231
  155.7 10.3 %convolution_bitcast_fusion.x_ref = f32[8,32,256]{2,1,0:T(8,128)} fusion(f32[32,2048,1]{1,0,2:T(8,128)S(1)} %reshape.138, bf16[8,256,2048]{2,1,0:T(8,128)(2,1)} %bitcast.116), kind=kOutput, calls=%fused_computation.26 | convolution fusion | flops 1610612736 | bytes 8912896 | tf_op jit(solution)/shard_map/dot_general | solution.py:231
  166.1 13.7 %shard_map.80 = f32[8,32,256]{2,1,0:T(8,128)} custom-call(f32[8,32,256]{2,1,0:T(8,128)} %convolution_bitcast_fusion.x_ref), custom_call_target="tpu_custom_call" | custom-call | tf_op jit(solution)/shard_map/pallas_call | solution.py:60
  181.5 10.7 %fusion.9 = f32[8,256,2048]{2,1,0:T(8,128)} fusion(bf16[8,256,2048]{2,1,0:T(8,128)(2,1)} %get-tuple-element.197, pred[256,256]{1,0:T(8,128)(4,1)S(1)} %iota_compare_fusion, bf16[8,256,16]{1,0,2:T(8,128)(2,1)S(1)} %get-tuple-element.204, bf16[8,256,16]{1,0,2:T(8,128)(2,1)S(1)} %get-tuple-element.203), kind=kOutput, calls=%fused_computation.25 | convolution fusion | flops 2165309440 | bytes 25362432 | tf_op jit(solution)/shard_map/jbc,jbe->jce/dot_general | solution.py:136
  192.2 11.9 %fusion = f32[8,256,2048]{2,1,0:T(8,128)} fusion(f32[8,256,2048]{2,1,0:T(8,128)} %fusion.9, f32[8,256]{1,0:T(8,128)S(1)} %multiply_bitcast_fusion.1, f32[256,2048]{1,0:T(8,128)S(1)} %multiply_exponential_fusion, f32[2048]{0:T(1024)S(1)} %negate_sqrt_fusion, bf16[8,256,16]{1,0,2:T(8,128)(2,1)S(1)} %get-tuple-element.203, ...), kind=kOutput, calls=%fused_computation.9 | convolution fusion | flops 156237824 | bytes 37044224 | tf_op jit(solution)/shard_map/jcn,jne->jce/dot_general | solution.py:136
  204.0 13.1 %fusion.4 = bf16[2048,2048]{1,0:T(8,128)(2,1)} fusion(f32[8,256,2048]{2,1,0:T(8,128)} %fusion, bf16[32,2048]{1,0:T(8,128)(2,1)S(1)} %copy-done, f32[2048]{0:T(1024)S(1)} %copy-done.4, bf16[2048,2048]{1,0:T(8,128)(2,1)} %param.15, bf16[32,2048]{1,0:T(8,128)(2,1)S(1)} %bitcast.134), kind=kOutput, calls=%fused_computation.15 | convolution fusion | flops 289406976 | bytes 33824768 | tf_op jit(solution)/shard_map/dot_general | solution.py:225
  (94 shorter events, 29.3 us)
Async XLA Ops:
  0.6 18.3 %copy-start = (bf16[32,2048]{1,0:T(8,128)(2,1)S(1)}, bf16[32,2048]{1,0:T(8,128)(2,1)}, u32[]{:S(2)}) copy-start(bf16[32,2048]{1,0:T(8,128)(2,1)} %param.11) | copy-start | bytes 393220
  2.2 16.7 %slice-start = ((s8[8388608]{0:T(1024)(128)(4,1)}), s8[4194304]{0:T(1024)(128)(4,1)S(1)}, s32[]{:S(2)}) async-start(s8[8388608]{0:T(1024)(128)(4,1)} %bitcast.113), calls=%async_computation | async-start | bytes 8388608
  4.2 14.8 %slice-start.1 = ((s8[8388608]{0:T(1024)(128)(4,1)}), s8[4194304]{0:T(1024)(128)(4,1)S(1)}, s32[]{:S(2)}) async-start(s8[8388608]{0:T(1024)(128)(4,1)} %bitcast.113), calls=%async_computation.1 | async-start | bytes 8388608
  112.6 1.3 copy-start.1
  115.3 6.1 %copy-start.2 = (f32[8,256,256]{2,1,0:T(8,128)S(1)}, f32[8,256,256]{2,1,0:T(8,128)}, u32[]{:S(2)}) copy-start(f32[8,256,256]{2,1,0:T(8,128)} %copy-done.1) | copy-start | bytes 6291460
  155.7 25.8 %copy-start.3 = (f32[4,32,512]{2,1,0:T(8,128)S(1)}, f32[4,32,512]{2,1,0:T(8,128)}, u32[]{:S(2)}) copy-start(f32[4,32,512]{2,1,0:T(8,128)} %shard_map.79) | copy-start | bytes 786436
  192.2 11.9 %copy-start.4 = (f32[2048]{0:T(1024)S(1)}, f32[2048]{0:T(1024)}, u32[]{:S(2)}) copy-start(f32[2048]{0:T(1024)} %param.14) | copy-start | bytes 24580

commit v2 on v1

v2 whole, which is shorter than its diff:
```python
import functools

import jax
import jax.numpy as jnp
from jax import lax
from jax.experimental import pallas as pl
from jax.experimental.pallas import tpu as pltpu
from jax.sharding import PartitionSpec as P

BLK = 256
MESH = pl.DeviceIdType.MESH


def greet(axis, n):
    me = lax.axis_index(axis)
    barrier = pltpu.get_barrier_semaphore()
    for k in range(1, n):
        pl.semaphore_signal(
            barrier, inc=1, device_id={axis: lax.rem(me + k, n)}, device_id_type=MESH
        )
    pl.semaphore_wait(barrier, n - 1)
    return me


def send(axis, n, me, k, src, dst, sems):
    copy = pltpu.make_async_remote_copy(
        src_ref=src,
        dst_ref=dst,
        send_sem=sems[0].at[k - 1],
        recv_sem=sems[1].at[k - 1],
        device_id={axis: lax.rem(me + k, n)},
        device_id_type=MESH,
    )
    copy.start()
    return copy


def reduce_kernel(axis, n, x_ref, o_ref, parts, total, s1, r1, s2, r2):
    me = greet(axis, n)
    copies = [
        send(axis, n, me, k, x_ref.at[lax.rem(me + k, n)], parts.at[k - 1], (s1, r1))
        for k in range(1, n)
    ]
    acc = x_ref[me]
    for k in range(1, n):
        copies[k - 1].wait_recv()
        acc = acc + parts[k - 1]
    total[me] = acc
    back = [send(axis, n, me, k, total.at[me], total.at[me], (s2, r2)) for k in range(1, n)]
    for copy in copies:
        copy.wait_send()
    for copy in back:
        copy.wait()
    o_ref[...] = total[...]


def reduced(x, axis, ident):
    n = x.shape[0]
    vmem = pl.BlockSpec(memory_space=pltpu.VMEM)
    return pl.pallas_call(
        functools.partial(reduce_kernel, axis, n),
        out_shape=jax.ShapeDtypeStruct(x.shape, x.dtype),
        in_specs=[vmem],
        out_specs=vmem,
        scratch_shapes=[
            pltpu.VMEM((n - 1,) + x.shape[1:], x.dtype),
            pltpu.VMEM(x.shape, x.dtype),
        ]
        + [pltpu.SemaphoreType.DMA((n - 1,))] * 4,
        compiler_params=pltpu.CompilerParams(collective_id=ident, has_side_effects=True),
    )(x)


def split(x, n):
    rows, length = x.shape
    return x.reshape(rows, n, length // n).transpose(1, 0, 2)


def join(x):
    n, rows, part = x.shape
    return x.transpose(1, 0, 2).reshape(rows, n * part)


def all_reduced(x, axis, ident):
    return join(reduced(split(x, lax.axis_size(axis)), axis, ident))


def scan_kernel(axis, n, nstate, x_ref, o_ref, got, out, home, s1, r1, s2, r2):
    me = greet(axis, n)
    copies = [
        send(axis, n, me, k, x_ref.at[lax.rem(me + k, n)], got.at[me], (s1, r1))
        for k in range(1, n)
    ]
    got[me] = x_ref[me]
    for copy in copies:
        copy.wait()
    zero = jnp.zeros((nstate, x_ref.shape[2]), jnp.float32)
    state = zero
    adjoint = zero
    for k in range(n):
        out[k, :nstate] = state
        state = got[k, :nstate] + got[k, 2 * nstate : 2 * nstate + 1] * state
        j = n - 1 - k
        out[j, nstate:] = adjoint
        adjoint = got[j, nstate : 2 * nstate] + got[j, 2 * nstate : 2 * nstate + 1] * adjoint
    back = [
        send(axis, n, me, k, out.at[lax.rem(me + k, n)], home.at[me], (s2, r2))
        for k in range(1, n)
    ]
    home[me] = out[me]
    for copy in back:
        copy.wait()
    o_ref[...] = home[...]


def scanned(x, nstate, axis, ident):
    n, rows, part = x.shape
    vmem = pl.BlockSpec(memory_space=pltpu.VMEM)
    small = (n, 2 * nstate, part)
    return pl.pallas_call(
        functools.partial(scan_kernel, axis, n, nstate),
        out_shape=jax.ShapeDtypeStruct(small, x.dtype),
        in_specs=[vmem],
        out_specs=vmem,
        scratch_shapes=[
            pltpu.VMEM(x.shape, x.dtype),
            pltpu.VMEM(small, x.dtype),
            pltpu.VMEM(small, x.dtype),
        ]
        + [pltpu.SemaphoreType.DMA((n - 1,))] * 4,
        compiler_params=pltpu.CompilerParams(collective_id=ident, has_side_effects=True),
    )(x)


def nt(left, right, **how):
    return lax.dot_general(
        left, right, (((1,), (1,)), ((), ())), preferred_element_type=jnp.float32, **how
    )


def tn(left, right):
    return lax.dot_general(
        left, right, (((0,), (0,)), ((), ())), preferred_element_type=jnp.float32
    )


def nn(left, right, **how):
    return jnp.dot(left, right, preferred_element_type=jnp.float32, **how)


def fill(rates_ref, scale_ref, base, inverse):
    offsets = lax.broadcasted_iota(jnp.int32, base.shape, 0).astype(jnp.float32) + 1.0
    base[...] = jnp.exp(-offsets * rates_ref[...])
    inverse[...] = scale_ref[...] / base[...]


def pieces(channels):
    width = 512 if channels % 512 == 0 else channels
    return [slice(at, at + width) for at in range(0, channels, width)]


def scaled_of(inner_ref, inverse, reach, cols):
    return (inner_ref[:, cols].astype(jnp.float32) * inverse[:, cols] * (1.0 / reach)).astype(jnp.bfloat16)


def weighted_of(upstream_ref, base, reach, cols):
    return (upstream_ref[:, cols].astype(jnp.float32) * (base[:, cols] * reach)).astype(jnp.bfloat16)


def lower():
    row = lax.broadcasted_iota(jnp.int32, (BLK, BLK), 0)
    col = lax.broadcasted_iota(jnp.int32, (BLK, BLK), 1)
    return row >= col


def cross_kernel(
    nstate, factor, inner, upstream, coef, reach_ref, rates, scale,
    cross, states, before, terms, pack, base, inverse,
):
    @pl.when(pl.program_id(0) == 0)
    def _():
        fill(rates, scale, base, inverse)
        pack[: 2 * nstate] = jnp.zeros_like(pack[: 2 * nstate])
        pack[2 * nstate :] = jnp.ones_like(pack[2 * nstate :])

    reach = reach_ref[...]
    short = coef[...].astype(jnp.bfloat16)
    write, read = short[:nstate], short[nstate:]
    total = jnp.zeros((BLK, BLK), jnp.float32)
    for cols in pieces(inner.shape[1]):
        scaled = scaled_of(inner, inverse, reach, cols)
        weighted = weighted_of(upstream, base, reach, cols)
        total = total + nt(weighted, scaled)
        decay = base[BLK - 1 :, cols] * reach[BLK - 1 :]
        state = pack[:nstate, cols]
        sofar = pack[2 * nstate :, cols]
        term = factor * nn(read, weighted)
        states[0, :, cols] = state
        before[0, :, cols] = sofar[:1]
        terms[0, :, cols] = term
        pack[:nstate, cols] = decay * state + decay * nn(write, scaled)
        pack[nstate : 2 * nstate, cols] = pack[nstate : 2 * nstate, cols] + sofar[:1] * term
        pack[2 * nstate :, cols] = sofar * decay
    cross[0] = jnp.where(lower(), total, 0.0)


def grad_kernel(
    nstate, factor, inner, upstream, coef, reach_ref, rates, scale,
    cross, states, before, terms, arrived, grad, carried_ref, base, inverse, adjoint,
):
    @pl.when(pl.program_id(0) == 0)
    def _():
        fill(rates, scale, base, inverse)
        adjoint[...] = arrived[nstate:]

    reach = reach_ref[...]
    exact = dict(precision=lax.Precision.HIGHEST)
    write_part = jnp.zeros((nstate, BLK), jnp.float32)
    read_part = jnp.zeros((nstate, BLK), jnp.float32)
    for cols in pieces(inner.shape[1]):
        scaled = scaled_of(inner, inverse, reach, cols)
        weighted = weighted_of(upstream, base, reach, cols)
        decay = base[BLK - 1 :, cols] * reach[BLK - 1 :]
        later = decay * adjoint[:, cols]
        carried = later.astype(jnp.bfloat16)
        adjoint[:, cols] = terms[0, :, cols] + later
        carried_ref[0, :, cols] = carried
        state = (states[0, :, cols] + before[0, :, cols] * arrived[:nstate, cols]).astype(jnp.bfloat16)
        write_part = write_part + nt(carried, scaled)
        read_part = read_part + nt(state, weighted)
    grad[:nstate] = factor * nn(coef[nstate:], cross[0], **exact) + write_part
    grad[nstate:] = factor * (read_part + nt(coef[:nstate], cross[0], **exact))


def final_kernel(
    nstate, factor, inner, upstream, coef, reach_ref, rates, scale,
    carried, grad, weight, skip, out, proj, base, inverse,
):
    @pl.when(pl.program_id(0) == 0)
    def _():
        fill(rates, scale, base, inverse)
        proj[...] = jnp.zeros_like(proj)

    reach = reach_ref[...]
    short = coef[...].astype(jnp.bfloat16)
    write, read = short[:nstate], short[nstate:]
    row = lax.broadcasted_iota(jnp.int32, (BLK, BLK), 0)
    col = lax.broadcasted_iota(jnp.int32, (BLK, BLK), 1)
    turned = jnp.where(col >= row, tn(write, read), 0.0).astype(jnp.bfloat16)
    full = grad[...]
    high = full.astype(jnp.bfloat16)
    rest = full - high.astype(jnp.float32)
    middle = rest.astype(jnp.bfloat16)
    low = (rest - middle.astype(jnp.float32)).astype(jnp.bfloat16)
    stack = jnp.concatenate([high, middle, low], axis=0)
    size = 2 * nstate
    for cols in pieces(inner.shape[1]):
        weighted = weighted_of(upstream, base, reach, cols)
        mixed = factor * nn(turned, weighted) + tn(write, carried[0, :, cols])
        value = inverse[:, cols] * (1.0 / reach) * mixed
        value = value + skip[:, cols] * upstream[:, cols].astype(jnp.float32)
        value = value + tn(high, weight[:, cols])
        out[:, cols] = value.astype(jnp.bfloat16)
        three = nn(stack, inner[:, cols])
        proj[:, cols] = proj[:, cols] + (three[:size] + (three[size : 2 * size] + three[2 * size :]))


def local(inner, proj_weight, rates, keep, skip, upstream):
    length, channels = inner.shape
    nstate = proj_weight.shape[0] // 2
    size = 2 * nstate
    nblocks = length // BLK
    f32 = jnp.float32
    partial_coef = nt(proj_weight, inner)
    coef = all_reduced(partial_coef, "fsdp", 0)
    factor = 1.0 / nstate**0.5
    scale = jnp.sqrt(-jnp.expm1(-2.0 * rates))[None]
    rates = rates[None]
    reach = jnp.cumprod(keep.reshape(nblocks, BLK), axis=1).reshape(length, 1)
    params = pltpu.CompilerParams(
        dimension_semantics=("arbitrary",), vmem_limit_bytes=48 * 2**20
    )

    def specs(turn):
        tokens = pl.BlockSpec((BLK, channels), lambda i: (turn(i), 0))
        coefs = pl.BlockSpec((size, BLK), lambda i: (0, turn(i)))
        column = pl.BlockSpec((BLK, 1), lambda i: (turn(i), 0))
        line = pl.BlockSpec((1, channels), lambda i: (0, 0))
        return tokens, coefs, column, line

    def per_block(turn, rows, width):
        return pl.BlockSpec((1, rows, width), lambda i: (turn(i), 0, 0))

    def whole(rows):
        return pl.BlockSpec((rows, channels), lambda i: (0, 0))

    def up(i):
        return i

    def down(i):
        return nblocks - 1 - i

    tables = [pltpu.VMEM((BLK, channels), f32)] * 2
    tokens, coefs, column, line = specs(up)
    shape = jax.ShapeDtypeStruct
    cross, states, before, terms, pack = pl.pallas_call(
        functools.partial(cross_kernel, nstate, factor),
        grid=(nblocks,),
        in_specs=[tokens, tokens, coefs, column, line, line],
        out_specs=[
            per_block(up, BLK, BLK),
            per_block(up, nstate, channels),
            per_block(up, 1, channels),
            per_block(up, nstate, channels),
            whole(size + 8),
        ],
        out_shape=[
            shape((nblocks, BLK, BLK), f32),
            shape((nblocks, nstate, channels), f32),
            shape((nblocks, 1, channels), f32),
            shape((nblocks, nstate, channels), f32),
            shape((size + 8, channels), f32),
        ],
        scratch_shapes=tables,
        compiler_params=params,
    )(inner, upstream, coef, reach, rates, scale)
    arrived = join(scanned(split(pack, lax.axis_size("ctx")), nstate, "ctx", 1))
    back_tokens, back_coefs, back_column, _ = specs(down)
    partial_grad, carried = pl.pallas_call(
        functools.partial(grad_kernel, nstate, factor),
        grid=(nblocks,),
        in_specs=[back_tokens, back_tokens, back_coefs, back_column, line, line]
        + [
            per_block(down, BLK, BLK),
            per_block(down, nstate, channels),
            per_block(down, 1, channels),
            per_block(down, nstate, channels),
            whole(size),
        ],
        out_specs=[back_coefs, per_block(down, nstate, channels)],
        out_shape=[
            shape((size, length), f32),
            shape((nblocks, nstate, channels), jnp.bfloat16),
        ],
        scratch_shapes=tables + [pltpu.VMEM((nstate, channels), f32)],
        compiler_params=params,
    )(inner, upstream, coef, reach, rates, scale, cross, states, before, terms, arrived)
    grad = all_reduced(partial_grad, "fsdp", 2)
    input_grad, proj = pl.pallas_call(
        functools.partial(final_kernel, nstate, factor),
        grid=(nblocks,),
        in_specs=[tokens, tokens, coefs, column, line, line]
        + [per_block(up, nstate, channels), coefs, whole(size), line],
        out_specs=[tokens, whole(size)],
        out_shape=[shape((length, channels), jnp.bfloat16), shape((size, channels), f32)],
        scratch_shapes=tables,
        compiler_params=params,
    )(inner, upstream, coef, reach, rates, scale, carried, grad, proj_weight, skip[None])
    total = all_reduced(proj, "ctx", 3)
    return (input_grad, total / (length * lax.axis_size("ctx")))


def solution(mesh):
    placed = (P("ctx", "fsdp"), P(None, "fsdp"), P("fsdp"), P("ctx"), P("fsdp"), P("ctx", "fsdp"))
    return jax.shard_map(
        local,
        mesh=mesh,
        in_specs=placed,
        out_specs=(P("ctx", "fsdp"), P(None, "fsdp")),
        check_vma=False,
    )
```

time: 218 us -> 128 us (0.59)
  matrix products: 83.1 us -> 6.04 us
  other arithmetic: 44.8 us -> 2.36 us
  Pallas kernels: 64 us -> 105 us
  local copies, waits for them, and re-layouts: 24 us -> 12.5 us
    dot_general x12 -> x1, matrix products: 83.1 us -> 6.04 us  [nt(): lax.dot_general(left, right, (((1,), (1,)), ((), ())), preferred_element_...]
    pallas_call x0 -> x3, Pallas kernels: none -> 41.1 us  [the longest x1 16.6 us: local(): pl.pallas_call(functools.partial(final_kernel, nstate, factor), grid=(nbl...]
    add x16 -> x0, other arithmetic: 15.6 us -> none  [the longest x8 7.81 us: forward(): return (item[0][None, :] * state + item[1], state)]
    convert_element_type x2 -> x0, other arithmetic: 14.6 us -> none  [the longest x1 14.6 us: local(): scaled = (input_scale[None, None, :] * inner.astype(jnp.float32).reshape(...]
    dot_general x1 -> x0, local copies, waits for them, and re-layouts: 12.2 us -> none  [local(): lax.dot_general(grad_coef, inner.astype(jnp.float32), (((0,), (0,)), ((),...]
    dynamic_update_slice x16 -> x0, other arithmetic: 10.6 us -> none  [local(): lax.scan(forward, zero_state, (decays, state_terms))]
    unnamed x18 -> x16, local copies, waits for them, and re-layouts: 2.32 us -> 4.68 us
    another operation x3 -> x1, local copies, waits for them, and re-layouts: 2.33 us -> 0.01 us
where the time goes in v2:
time: 128 us; the launch traced here: 127 us
  Pallas kernels  105 us (82%)
  local copies, waits for them, and re-layouts  12.5 us (10%)
  matrix products  6.04 us (5%)
  other arithmetic  2.36 us (2%)
    pallas_call x3, Pallas kernels, reduced(): pl.pallas_call(functools.partial(reduce_kernel, axis, n), out_shape=jax.S...  49.9 us
    pallas_call x1, Pallas kernels, local(): pl.pallas_call(functools.partial(final_kernel, nstate, factor), grid=(nbl...  16.6 us
    pallas_call x1, Pallas kernels, scanned(): pl.pallas_call(functools.partial(scan_kernel, axis, n, nstate), out_shape...  14.1 us
    pallas_call x1, Pallas kernels, local(): pl.pallas_call(functools.partial(grad_kernel, nstate, factor), grid=(nblo...  12.7 us
    pallas_call x1, Pallas kernels, local(): pl.pallas_call(functools.partial(cross_kernel, nstate, factor), grid=(nbl...  11.8 us
    dot_general x1, matrix products, nt(): lax.dot_general(left, right, (((1,), (1,)), ((), ())), preferred_element_...  6.04 us
    unnamed x16, local copies, waits for them, and re-layouts  4.68 us
    reshape x4, local copies, waits for them, and re-layouts, split(): return x.reshape(rows, n, length // n).transpose(1, 0, 2)  2.92 us

profile of v2, /device:TPU:0, one launch (start us, length us, event | category | flops | bytes accessed | tf_op | source)
XLA Modules:
  0.0 126.8 jit_solution(14170640855453886591)
XLA Ops:
  0.6 0.0 copy-start.4
  0.6 0.7 copy.14
  1.3 0.6 reduce-window.6
  1.9 0.2 slice_reduce_fusion
  2.1 0.1 broadcast_multiply_fusion
  2.2 0.7 negate_sqrt_fusion
  2.9 6.0 %fusion = f32[32,2048]{1,0:T(8,128)S(1)} fusion(bf16[32,2048]{1,0:T(8,128)(2,1)} %weight.1, bf16[2048,2048]{1,0:T(8,128)(2,1)} %inner.5), kind=kOutput, calls=%fused_computation.8 | convolution fusion | flops 268435456 | bytes 8781824 | tf_op jit(solution)/shard_map/dot_general | solution.py:136
  9.0 0.7 copy.40
  9.7 18.2 %shard_map.77 = f32[4,32,512]{2,1,0:T(8,128)} custom-call(f32[4,32,512]{2,1,0:T(8,128)} %bitcast.65), custom_call_target="tpu_custom_call" | custom-call | tf_op jit(solution)/shard_map/pallas_call | solution.py:60
  27.9 1.0 copy.29
  28.9 0.4 copy.22.reach_ref
  29.3 11.8 %shard_map.78 = (f32[8,256,256]{2,1,0:T(8,128)S(1)}, f32[8,16,2048]{2,1,0:T(8,128)S(1)}, f32[8,1,2048]{2,1,0:T(1,128)S(1)}, f32[8,16,2048]{2,1,0:T(8,128)S(1)}, f32[40,2048]{1,0:T(8,128)S(1)}) custom-call(bf16[2048,2048]{1,0:T(8,128)(2,1)} %inner.5, bf16[2048,2048]{1,0:T(8,128)(2,1)} %upstream.5, f32[32,2048]{1,0:T(8,128)S(1)} %bitcast.48, ...), custom_call_target="tpu_custom_call" | custom-call | tf_op jit(solution)/shard_map/pallas_call | solution.py:306
  41.1 0.0 copy-start
  41.1 1.3 %copy-done = f32[8,256,256]{2,1,0:T(8,128)} copy-done((f32[8,256,256]{2,1,0:T(8,128)}, f32[8,256,256]{2,1,0:T(8,128)S(1)}, u32[]{:S(2)}) %copy-start) | copy-done | bytes 2097176
  42.4 0.7 copy.37
  43.1 14.1 %shard_map.79 = f32[8,32,256]{2,1,0:T(8,128)} custom-call(f32[8,40,256]{2,1,0:T(8,128)} %bitcast.63), custom_call_target="tpu_custom_call" | custom-call | tf_op jit(solution)/shard_map/pallas_call | solution.py:120
  57.2 1.0 copy.30
  58.2 0.0 copy-start.6
  58.2 0.8 copy-done.6
  59.1 12.7 %shard_map.80 = (f32[32,2048]{1,0:T(8,128)S(1)}, bf16[8,16,2048]{2,1,0:T(8,128)(2,1)S(1)}) custom-call(bf16[2048,2048]{1,0:T(8,128)(2,1)} %inner.5, bf16[2048,2048]{1,0:T(8,128)(2,1)} %upstream.5, f32[32,2048]{1,0:T(8,128)S(1)} %bitcast.49, f32[2048,1]{1,0:T(8,128)S(1)} %copy.22.reach_ref, f32[1,2048]{1,0:T(1,128)S(1)} %bitcast.57, f32[1,2048]{1,0:T(1,128)S(1)} %bitcast.60, ...), custom_call_target="tpu_custom_call" | custom-call | tf_op jit(solution)/shard_map/pallas_call | solution.py:329
  71.8 0.0 copy-start.2
  71.8 0.8 copy-done.2
  72.6 0.7 copy.39
  73.3 18.0 %shard_map.81 = f32[4,32,512]{2,1,0:T(8,128)} custom-call(f32[4,32,512]{2,1,0:T(8,128)} %bitcast.68), custom_call_target="tpu_custom_call" | custom-call | tf_op jit(solution)/shard_map/pallas_call | solution.py:60
  91.3 1.0 copy.31
  92.3 1.0 copy-done.3
  93.3 0.7 copy-done.7
  94.0 16.6 %shard_map.82 = (bf16[2048,2048]{1,0:T(8,128)(2,1)}, f32[32,2048]{1,0:T(8,128)S(1)}) custom-call(bf16[2048,2048]{1,0:T(8,128)(2,1)} %inner.5, bf16[2048,2048]{1,0:T(8,128)(2,1)} %upstream.5, f32[32,2048]{1,0:T(8,128)S(1)} %bitcast.50, f32[2048,1]{1,0:T(8,128)S(1)} %copy.22.reach_ref, f32[1,2048]{1,0:T(1,128)S(1)} %bitcast.58, f32[1,2048]{1,0:T(1,128)S(1)} %bitcast.61, ...), custom_call_target="tpu_custom_call" | custom-call | tf_op jit(solution)/shard_map/pallas_call | solution.py:349
  110.6 0.7 copy.38
  111.4 13.7 %shard_map.83 = f32[8,32,256]{2,1,0:T(8,128)} custom-call(f32[8,32,256]{2,1,0:T(8,128)} %bitcast.70), custom_call_target="tpu_custom_call" | custom-call | tf_op jit(solution)/shard_map/pallas_call | solution.py:60
  125.1 1.0 multiply_bitcast_fusion
  126.0 0.7 copy.32
  (10 shorter events, 0.1 us)
Async XLA Ops:
  0.6 28.7 %copy-start.4 = (f32[2048]{0:T(1024)S(1)}, f32[2048]{0:T(1024)}, u32[]{:S(2)}) copy-start(f32[2048]{0:T(1024)} %param.8) | copy-start | bytes 24580
  41.1 1.3 %copy-start = (f32[8,256,256]{2,1,0:T(8,128)}, f32[8,256,256]{2,1,0:T(8,128)S(1)}, u32[]{:S(2)}) copy-start(f32[8,256,256]{2,1,0:T(8,128)S(1)} %get-tuple-element.11.cross) | copy-start | bytes 6291460
  42.4 15.8 %copy-start.5 = (f32[8,1,2048]{2,1,0:T(1,128)}, f32[8,1,2048]{2,1,0:T(1,128)S(1)}, u32[]{:S(2)}) copy-start(f32[8,1,2048]{2,1,0:T(1,128)S(1)} %get-tuple-element.13.before) | copy-start | bytes 196612
  58.2 0.8 copy-start.6
  59.1 33.2 %copy-start.1 = (bf16[32,2048]{1,0:T(8,128)(2,1)S(1)}, bf16[32,2048]{1,0:T(8,128)(2,1)}, u32[]{:S(2)}) copy-start(bf16[32,2048]{1,0:T(8,128)(2,1)} %weight.1) | copy-start | bytes 393220
  71.8 0.8 copy-start.2
  92.3 1.0 copy-start.3
  93.3 0.7 copy-start.7

commit v3 on v2

v3 whole, which is shorter than its diff:
```python
import functools

import jax
import jax.numpy as jnp
from jax import lax
from jax.experimental import pallas as pl
from jax.experimental.pallas import tpu as pltpu
from jax.sharding import PartitionSpec as P

BLK = 256
MESH = pl.DeviceIdType.MESH


def greet(axis, n):
    me = lax.axis_index(axis)
    barrier = pltpu.get_barrier_semaphore()
    for k in range(1, n):
        pl.semaphore_signal(
            barrier, inc=1, device_id={axis: lax.rem(me + k, n)}, device_id_type=MESH
        )
    pl.semaphore_wait(barrier, n - 1)
    return me


def send(axis, n, me, k, src, dst, sems):
    copy = pltpu.make_async_remote_copy(
        src_ref=src,
        dst_ref=dst,
        send_sem=sems[0].at[k - 1],
        recv_sem=sems[1].at[k - 1],
        device_id={axis: lax.rem(me + k, n)},
        device_id_type=MESH,
    )
    copy.start()
    return copy


def reduce_kernel(axis, n, x_ref, o_ref, parts, total, s1, r1, s2, r2):
    me = greet(axis, n)
    copies = [
        send(axis, n, me, k, x_ref.at[lax.rem(me + k, n)], parts.at[k - 1], (s1, r1))
        for k in range(1, n)
    ]
    acc = x_ref[me]
    for k in range(1, n):
        copies[k - 1].wait_recv()
        acc = acc + parts[k - 1]
    total[me] = acc
    back = [send(axis, n, me, k, total.at[me], total.at[me], (s2, r2)) for k in range(1, n)]
    for copy in copies:
        copy.wait_send()
    for copy in back:
        copy.wait()
    o_ref[...] = total[...]


def reduced(x, axis, ident):
    n = x.shape[0]
    vmem = pl.BlockSpec(memory_space=pltpu.VMEM)
    return pl.pallas_call(
        functools.partial(reduce_kernel, axis, n),
        out_shape=jax.ShapeDtypeStruct(x.shape, x.dtype),
        in_specs=[vmem],
        out_specs=vmem,
        scratch_shapes=[
            pltpu.VMEM((n - 1,) + x.shape[1:], x.dtype),
            pltpu.VMEM(x.shape, x.dtype),
        ]
        + [pltpu.SemaphoreType.DMA((n - 1,))] * 4,
        compiler_params=pltpu.CompilerParams(collective_id=ident, has_side_effects=True),
    )(x)


def split(x, n):
    rows, length = x.shape
    return x.reshape(rows, n, length // n).transpose(1, 0, 2)


def join(x):
    n, rows, part = x.shape
    return x.transpose(1, 0, 2).reshape(rows, n * part)


def all_reduced(x, axis, ident):
    return join(reduced(split(x, lax.axis_size(axis)), axis, ident))


def nt(left, right, **how):
    return lax.dot_general(
        left, right, (((1,), (1,)), ((), ())), preferred_element_type=jnp.float32, **how
    )


def tn(left, right):
    return lax.dot_general(
        left, right, (((0,), (0,)), ((), ())), preferred_element_type=jnp.float32
    )


def nn(left, right, **how):
    return jnp.dot(left, right, preferred_element_type=jnp.float32, **how)


def fill(rates_ref, scale_ref, base, inverse):
    offsets = lax.broadcasted_iota(jnp.int32, base.shape, 0).astype(jnp.float32) + 1.0
    base[...] = jnp.exp(-offsets * rates_ref[...])
    inverse[...] = scale_ref[...] / base[...]


def pieces(channels):
    width = 512 if channels % 512 == 0 else channels
    return [slice(at, at + width) for at in range(0, channels, width)]


def scaled_of(inner_ref, inverse, reach, cols):
    return (inner_ref[:, cols].astype(jnp.float32) * inverse[:, cols] * (1.0 / reach)).astype(jnp.bfloat16)


def weighted_of(upstream_ref, base, reach, cols):
    return (upstream_ref[:, cols].astype(jnp.float32) * (base[:, cols] * reach)).astype(jnp.bfloat16)


def lower():
    row = lax.broadcasted_iota(jnp.int32, (BLK, BLK), 0)
    col = lax.broadcasted_iota(jnp.int32, (BLK, BLK), 1)
    return row >= col


def copy_to(axis, n, me, k, src, dst, sems):
    return pltpu.make_async_remote_copy(
        src_ref=src,
        dst_ref=dst,
        send_sem=sems[0].at[k - 1],
        recv_sem=sems[1].at[k - 1],
        device_id={axis: lax.rem(me + k, n)},
        device_id_type=MESH,
    )


def scatters(n, me, part, got, sems):
    per = part.shape[0] // n
    return [
        copy_to(
            "fsdp", n, me, k, part.at[pl.ds(lax.rem(me + k, n) * per, per)], got.at[k - 1], sems
        )
        for k in range(1, n)
    ]


def gathers(n, me, total, sems):
    per = total.shape[0] // n
    own = total.at[pl.ds(me * per, per)]
    return [copy_to("fsdp", n, me, k, own, own, sems) for k in range(1, n)]


def summed(n, me, part, got, total, sems):
    per = part.shape[0] // n
    acc = part[pl.ds(me * per, per)]
    for k, copy in enumerate(scatters(n, me, part, got, sems)):
        copy.wait()
        acc = acc + got[k]
    total[pl.ds(me * per, per)] = acc


def main_kernel(
    nstate, factor, nblocks, nf, nc,
    inner, upstream, weight, reach_ref, rates, scale,
    coef_out, grad_out, carried_ref,
    base, inverse, scaled_all, weighted_all, cross, part, got, coef, gpart, ggot, grad,
    states, before, terms, pack, packed, arriving, leaving, home, arrived, adjoint,
    s1, r1, s2, r2, s3, r3, s4, r4, s5, r5, s6, r6,
):
    step = pl.program_id(0)
    size = 2 * nstate
    channels = inner.shape[1]
    width = channels // nc
    f = lax.axis_index("fsdp")
    c = lax.axis_index("ctx")
    barrier = pltpu.get_barrier_semaphore()

    @pl.when(step == 0)
    def _():
        for axis, n, me in (("fsdp", nf, f), ("ctx", nc, c)):
            for k in range(1, n):
                pl.semaphore_signal(
                    barrier, inc=1, device_id={axis: lax.rem(me + k, n)}, device_id_type=MESH
                )
        fill(rates, scale, base, inverse)
        pack[:size] = jnp.zeros_like(pack[:size])
        pack[size:] = jnp.ones_like(pack[size:])

    @pl.when(step < nblocks)
    def _():
        part[step] = nt(weight[...], inner[...])
        for cols in pieces(channels):
            scaled_all[step, :, cols] = scaled_of(inner, inverse, reach_ref[step], cols)

    @pl.when(step == nblocks)
    def _():
        pl.semaphore_wait(barrier, nf + nc - 2)
        for copy in scatters(nf, f, part, got, (s1, r1)):
            copy.start()

    @pl.when(step == nblocks + nblocks // 2)
    def _():
        summed(nf, f, part, got, coef, (s1, r1))
        for copy in gathers(nf, f, coef, (s2, r2)):
            copy.start()

    @pl.when(step >= nblocks)
    def _():
        j = step - nblocks
        total = jnp.zeros((BLK, BLK), jnp.float32)
        for cols in pieces(channels):
            weighted = weighted_of(upstream, base, reach_ref[j], cols)
            weighted_all[j, :, cols] = weighted
            total = total + nt(weighted, scaled_all[j, :, cols])
        cross[j] = jnp.where(lower(), total, 0.0)

    @pl.when(step == 2 * nblocks - 1)
    def _():
        for copy in gathers(nf, f, coef, (s2, r2)):
            copy.wait()

        def local_states(j, carry):
            short = coef[j].astype(jnp.bfloat16)
            write, read = short[:nstate], short[nstate:]
            for cols in pieces(channels):
                decay = base[BLK - 1 :, cols] * reach_ref[j, BLK - 1 :]
                state = pack[:nstate, cols]
                sofar = pack[size:, cols]
                term = factor * nn(read, weighted_all[j, :, cols])
                states[j, :, cols] = state
                before[j, :, cols] = sofar[:1]
                terms[j, :, cols] = term
                pack[:nstate, cols] = decay * state + decay * nn(write, scaled_all[j, :, cols])
                pack[nstate:size, cols] = pack[nstate:size, cols] + sofar[:1] * term
                pack[size:, cols] = sofar * decay
            return carry

        lax.fori_loop(0, nblocks, local_states, 0)
        for d in range(nc):
            packed[d] = pack[:, d * width : (d + 1) * width]
        out = [
            copy_to("ctx", nc, c, k, packed.at[lax.rem(c + k, nc)], arriving.at[c], (s3, r3))
            for k in range(1, nc)
        ]
        for copy in out:
            copy.start()
        arriving[c] = packed[c]
        for copy in out:
            copy.wait()
        state = jnp.zeros((nstate, width), jnp.float32)
        later = state
        for k in range(nc):
            leaving[k, :nstate] = state
            state = arriving[k, :nstate] + arriving[k, size : size + 1] * state
            j = nc - 1 - k
            leaving[j, nstate:] = later
            later = arriving[j, nstate:size] + arriving[j, size : size + 1] * later
        back = [
            copy_to("ctx", nc, c, k, leaving.at[lax.rem(c + k, nc)], home.at[c], (s4, r4))
            for k in range(1, nc)
        ]
        for copy in back:
            copy.start()
        home[c] = leaving[c]
        for copy in back:
            copy.wait()
        for d in range(nc):
            arrived[:, d * width : (d + 1) * width] = home[d]
        adjoint[...] = arrived[nstate:]
        exact = dict(precision=lax.Precision.HIGHEST)

        def local_grads(k, carry):
            j = nblocks - 1 - k
            write_part = jnp.zeros((nstate, BLK), jnp.float32)
            read_part = jnp.zeros((nstate, BLK), jnp.float32)
            for cols in pieces(channels):
                decay = base[BLK - 1 :, cols] * reach_ref[j, BLK - 1 :]
                later = decay * adjoint[:, cols]
                carried = later.astype(jnp.bfloat16)
                adjoint[:, cols] = terms[j, :, cols] + later
                carried_ref[j, :, cols] = carried
                state = states[j, :, cols] + before[j, :, cols] * arrived[:nstate, cols]
                write_part = write_part + nt(carried, scaled_all[j, :, cols])
                read_part = read_part + nt(state.astype(jnp.bfloat16), weighted_all[j, :, cols])
            wide = coef[j]
            gpart[j, :nstate] = factor * nn(wide[nstate:], cross[j], **exact) + write_part
            gpart[j, nstate:] = factor * (read_part + nt(wide[:nstate], cross[j], **exact))
            return carry

        lax.fori_loop(0, nblocks, local_grads, 0)
        for copy in scatters(nf, f, gpart, ggot, (s5, r5)):
            copy.start()
        coef_out[...] = coef[...]
        summed(nf, f, gpart, ggot, grad, (s5, r5))
        final = gathers(nf, f, grad, (s6, r6))
        for copy in final:
            copy.start()
        for copy in final:
            copy.wait()
        grad_out[...] = grad[...]


def final_kernel(
    nstate, factor, inner, upstream, coef, reach_ref, rates, scale,
    carried, grad, weight, skip, out, proj, base, inverse,
):
    @pl.when(pl.program_id(0) == 0)
    def _():
        fill(rates, scale, base, inverse)
        proj[...] = jnp.zeros_like(proj)

    reach = reach_ref[...]
    short = coef[0].astype(jnp.bfloat16)
    write, read = short[:nstate], short[nstate:]
    row = lax.broadcasted_iota(jnp.int32, (BLK, BLK), 0)
    col = lax.broadcasted_iota(jnp.int32, (BLK, BLK), 1)
    turned = jnp.where(col >= row, tn(write, read), 0.0).astype(jnp.bfloat16)
    full = grad[0]
    high = full.astype(jnp.bfloat16)
    rest = full - high.astype(jnp.float32)
    middle = rest.astype(jnp.bfloat16)
    low = (rest - middle.astype(jnp.float32)).astype(jnp.bfloat16)
    stack = jnp.concatenate([high, middle, low], axis=0)
    size = 2 * nstate
    for cols in pieces(inner.shape[1]):
        weighted = weighted_of(upstream, base, reach, cols)
        mixed = factor * nn(turned, weighted) + tn(write, carried[0, :, cols])
        value = inverse[:, cols] * (1.0 / reach) * mixed
        value = value + skip[:, cols] * upstream[:, cols].astype(jnp.float32)
        value = value + tn(high, weight[:, cols])
        out[:, cols] = value.astype(jnp.bfloat16)
        three = nn(stack, inner[:, cols])
        proj[:, cols] = proj[:, cols] + (three[:size] + (three[size : 2 * size] + three[2 * size :]))


def local(inner, proj_weight, rates, keep, skip, upstream):
    length, channels = inner.shape
    nstate = proj_weight.shape[0] // 2
    size = 2 * nstate
    nblocks = length // BLK
    f32 = jnp.float32
    factor = 1.0 / nstate**0.5
    scale = jnp.sqrt(-jnp.expm1(-2.0 * rates))[None]
    rates = rates[None]
    reach = jnp.cumprod(keep.reshape(nblocks, BLK), axis=1).reshape(length, 1)
    params = pltpu.CompilerParams(
        dimension_semantics=("arbitrary",), vmem_limit_bytes=48 * 2**20
    )

    nf, nc = lax.axis_size("fsdp"), lax.axis_size("ctx")
    bf16 = jnp.bfloat16
    whole = pl.BlockSpec(memory_space=pltpu.VMEM)
    shape = jax.ShapeDtypeStruct
    tables = [pltpu.VMEM((BLK, channels), f32)] * 2
    coefs = (nblocks, size, BLK)
    got = pltpu.VMEM((nf - 1, nblocks // nf, size, BLK), f32)
    entry = (nblocks, nstate, channels)
    width = channels // nc
    scratch = (
        tables
        + [pltpu.VMEM((nblocks, BLK, channels), bf16)] * 2
        + [pltpu.VMEM((nblocks, BLK, BLK), f32)]
        + [pltpu.VMEM(coefs, f32), got, pltpu.VMEM(coefs, f32)] * 2
        + [pltpu.VMEM(entry, f32), pltpu.VMEM((nblocks, 1, channels), f32), pltpu.VMEM(entry, f32)]
        + [pltpu.VMEM((size + 8, channels), f32)]
        + [pltpu.VMEM((nc, size + 8, width), f32)] * 2
        + [pltpu.VMEM((nc, size, width), f32)] * 2
        + [pltpu.VMEM((size, channels), f32), pltpu.VMEM((nstate, channels), f32)]
        + [pltpu.SemaphoreType.DMA((nf - 1,))] * 4
        + [pltpu.SemaphoreType.DMA((nc - 1,))] * 4
        + [pltpu.SemaphoreType.DMA((nf - 1,))] * 4
    )
    coef, grad, carried = pl.pallas_call(
        functools.partial(main_kernel, nstate, factor, nblocks, nf, nc),
        grid=(2 * nblocks,),
        in_specs=[
            pl.BlockSpec((BLK, channels), lambda i: (jnp.minimum(i, nblocks - 1), 0)),
            pl.BlockSpec((BLK, channels), lambda i: (jnp.maximum(i - nblocks, 0), 0)),
            whole, whole, whole, whole,
        ],
        out_specs=[whole, whole, whole],
        out_shape=[shape(coefs, f32), shape(coefs, f32), shape(entry, bf16)],
        scratch_shapes=scratch,
        compiler_params=pltpu.CompilerParams(
            dimension_semantics=("arbitrary",),
            vmem_limit_bytes=56 * 2**20,
            collective_id=0,
            has_side_effects=True,
        ),
    )(inner, upstream, proj_weight, reach.reshape(nblocks, BLK, 1), rates, scale)

    tokens = pl.BlockSpec((BLK, channels), lambda i: (i, 0))
    column = pl.BlockSpec((BLK, 1), lambda i: (i, 0))
    line = pl.BlockSpec((1, channels), lambda i: (0, 0))
    fixed = pl.BlockSpec((size, channels), lambda i: (0, 0))
    block_coef = pl.BlockSpec((1, size, BLK), lambda i: (i, 0, 0))
    block_state = pl.BlockSpec((1, nstate, channels), lambda i: (i, 0, 0))
    input_grad, proj = pl.pallas_call(
        functools.partial(final_kernel, nstate, factor),
        grid=(nblocks,),
        in_specs=[tokens, tokens, block_coef, column, line, line]
        + [block_state, block_coef, fixed, line],
        out_specs=[tokens, fixed],
        out_shape=[shape((length, channels), bf16), shape((size, channels), f32)],
        scratch_shapes=tables,
        compiler_params=params,
    )(inner, upstream, coef, reach, rates, scale, carried, grad, proj_weight, skip[None])
    total = all_reduced(proj, "ctx", 1)
    return (input_grad, total / (length * nc))


def solution(mesh):
    placed = (P("ctx", "fsdp"), P(None, "fsdp"), P("fsdp"), P("ctx"), P("fsdp"), P("ctx", "fsdp"))
    return jax.shard_map(
        local,
        mesh=mesh,
        in_specs=placed,
        out_specs=(P("ctx", "fsdp"), P(None, "fsdp")),
        check_vma=False,
    )
```

time: 128 us -> 102 us (0.80)
  Pallas kernels: 105 us -> 90 us
  matrix products: 6.04 us -> 0 us
  local copies, waits for them, and re-layouts: 12.5 us -> 6.98 us
    pallas_call x3 -> x1, Pallas kernels: 49.9 us -> 13.2 us  [reduced(): pl.pallas_call(functools.partial(reduce_kernel, axis, n), out_shape=jax.S...]
    pallas_call x3 -> x1, Pallas kernels: 38.6 us -> 60.1 us  [local(): pl.pallas_call(functools.partial(main_kernel, nstate, factor, nblocks, nf...]
    dot_general x1 -> x0, matrix products: 6.04 us -> none  [nt(): lax.dot_general(left, right, (((1,), (1,)), ((), ())), preferred_element_...]
    reshape x4 -> x1, local copies, waits for them, and re-layouts: 3.61 us -> 0.7 us  [the longest x3 2.91 us: join(): return x.transpose(1, 0, 2).reshape(rows, n * part)]
    reshape x4 -> x1, local copies, waits for them, and re-layouts: 2.92 us -> 0.72 us  [split(): return x.reshape(rows, n, length // n).transpose(1, 0, 2)]
    unnamed x16 -> x14, local copies, waits for them, and re-layouts: 4.68 us -> 2.95 us
    mul x2 -> x3, local copies, waits for them, and re-layouts: 0.37 us -> 1.72 us
where the time goes in v3:
time: 102 us; the launch traced here: 101 us
  Pallas kernels  90 us (88%)
  local copies, waits for them, and re-layouts  6.98 us (7%)
  other arithmetic  3.04 us (3%)
    pallas_call x1, Pallas kernels, local(): pl.pallas_call(functools.partial(main_kernel, nstate, factor, nblocks, nf...  60.1 us
    pallas_call x1, Pallas kernels, local(): pl.pallas_call(functools.partial(final_kernel, nstate, factor), grid=(nbl...  16.7 us
    pallas_call x1, Pallas kernels, reduced(): pl.pallas_call(functools.partial(reduce_kernel, axis, n), out_shape=jax.S...  13.2 us
    unnamed x14, local copies, waits for them, and re-layouts  2.95 us

profile of v3, /device:TPU:0, one launch (start us, length us, event | category | flops | bytes accessed | tf_op | source)
XLA Modules:
  0.0 100.7 jit_solution(10332015467006523693)
XLA Ops:
  0.6 0.7 copy.10
  1.3 0.6 reduce-window.6
  1.9 0.2 slice_reduce_fusion
  2.1 0.1 fusion
  2.2 0.1 broadcast_multiply_fusion
  2.3 1.3 %negate_sqrt_fusion = f32[2048]{0:T(1024)} fusion(f32[2048]{0:T(1024)} %param.8), kind=kLoop, calls=%fused_computation.3 | loop fusion | flops 4096 | bytes 16384 | tf_op jit(solution)/shard_map/sqrt | solution.py:346
  3.6 0.4 copy.13.reach_ref
  3.9 1.4 %copy.11.reach_ref = f32[8,256,1]{2,1,0:T(8,128)} copy(f32[8,256,1]{1,0,2:T(8,128)S(1)} %fusion) | data formatting | bytes 16384 | tf_op jit(solution)/shard_map/mul
  5.3 0.0 copy-start
  5.3 0.0 copy-start.4
  5.3 0.0 copy-start.5
  5.3 0.0 copy-start.6
  5.3 60.1 %shard_map.77 = (f32[8,32,256]{2,1,0:T(8,128)}, f32[8,32,256]{2,1,0:T(8,128)}, bf16[8,16,2048]{2,1,0:T(8,128)(2,1)}) custom-call(bf16[2048,2048]{1,0:T(8,128)(2,1)} %inner.3, bf16[2048,2048]{1,0:T(8,128)(2,1)} %upstream.3, bf16[32,2048]{1,0:T(8,128)(2,1)} %weight.3, f32[8,256,1]{2,1,0:T(8,128)} %copy.11.reach_ref, f32[1,2048]{1,0:T(1,128)} %bitcast.19, ...), custom_call_target="tpu_custom_call" | custom-call | tf_op jit(solution)/shard_map/pallas_call | solution.py:376
  65.4 0.0 copy-done
  65.4 0.0 copy-done.4
  65.4 0.0 copy-done.5
  65.5 0.0 copy-done.6
  65.5 0.0 copy-start.1
  65.5 1.0 %copy-done.1 = bf16[8,16,2048]{2,1,0:T(8,128)(2,1)S(1)} copy-done((bf16[8,16,2048]{2,1,0:T(8,128)(2,1)S(1)}, bf16[8,16,2048]{2,1,0:T(8,128)(2,1)}, u32[]{:S(2)}) %copy-start.1) | copy-done | bytes 524312
  66.5 0.0 copy-start.2
  66.5 0.9 copy-done.2
  67.5 0.0 copy-start.3
  67.5 0.9 copy-done.3
  68.4 16.7 %shard_map.78 = (bf16[2048,2048]{1,0:T(8,128)(2,1)}, f32[32,2048]{1,0:T(8,128)S(1)}) custom-call(bf16[2048,2048]{1,0:T(8,128)(2,1)} %inner.3, bf16[2048,2048]{1,0:T(8,128)(2,1)} %upstream.3, f32[8,32,256]{2,1,0:T(8,128)S(1)} %copy-done.2, f32[2048,1]{1,0:T(8,128)S(1)} %copy.13.reach_ref, f32[1,2048]{1,0:T(1,128)S(1)} %bitcast.20, f32[1,2048]{1,0:T(1,128)S(1)} %bitcast.22, ...), custom_call_target="tpu_custom_call" | custom-call | tf_op jit(solution)/shard_map/pallas_call | solution.py:401
  85.1 0.7 copy.19
  85.8 13.2 %shard_map.79 = f32[8,32,256]{2,1,0:T(8,128)} custom-call(f32[8,32,256]{2,1,0:T(8,128)} %bitcast.24), custom_call_target="tpu_custom_call" | custom-call | tf_op jit(solution)/shard_map/pallas_call | solution.py:60
  99.0 1.0 multiply_bitcast_fusion
  100.0 0.7 copy.17
  (3 shorter events, 0.1 us)
Async XLA Ops:
  5.3 60.1 %copy-start = (bf16[32,2048]{1,0:T(8,128)(2,1)S(1)}, bf16[32,2048]{1,0:T(8,128)(2,1)}, u32[]{:S(2)}) copy-start(bf16[32,2048]{1,0:T(8,128)(2,1)} %weight.3) | copy-start | bytes 393220
  5.3 60.1 %copy-start.4 = (f32[2048]{0:T(1024)S(1)}, f32[2048]{0:T(1024)}, u32[]{:S(2)}) copy-start(f32[2048]{0:T(1024)} %param.8) | copy-start | bytes 24580
  5.3 60.2 %copy-start.5 = (f32[2048]{0:T(1024)S(1)}, f32[2048]{0:T(1024)}, u32[]{:S(2)}) copy-start(f32[2048]{0:T(1024)} %negate_sqrt_fusion) | copy-start | bytes 24580
  5.3 60.2 %copy-start.6 = (f32[2048]{0:T(1024)S(1)}, f32[2048]{0:T(1024)}, u32[]{:S(2)}) copy-start(f32[2048]{0:T(1024)} %param.10) | copy-start | bytes 24580
  65.5 1.0 %copy-start.1 = (bf16[8,16,2048]{2,1,0:T(8,128)(2,1)S(1)}, bf16[8,16,2048]{2,1,0:T(8,128)(2,1)}, u32[]{:S(2)}) copy-start(bf16[8,16,2048]{2,1,0:T(8,128)(2,1)} %get-tuple-element.8.carried) | copy-start | bytes 1572868
  66.5 0.9 copy-start.2
  67.5 0.9 copy-start.3

commit v4 on v3

--- a/solution.py
+++ b/solution.py
@@ -9,80 +9,6 @@
 
 BLK = 256
 MESH = pl.DeviceIdType.MESH
-
-
-def greet(axis, n):
-    me = lax.axis_index(axis)
-    barrier = pltpu.get_barrier_semaphore()
-    for k in range(1, n):
-        pl.semaphore_signal(
-            barrier, inc=1, device_id={axis: lax.rem(me + k, n)}, device_id_type=MESH
-        )
-    pl.semaphore_wait(barrier, n - 1)
-    return me
-
-
-def send(axis, n, me, k, src, dst, sems):
-    copy = pltpu.make_async_remote_copy(
-        src_ref=src,
-        dst_ref=dst,
-        send_sem=sems[0].at[k - 1],
-        recv_sem=sems[1].at[k - 1],
-        device_id={axis: lax.rem(me + k, n)},
-        device_id_type=MESH,
-    )
-    copy.start()
-    return copy
-
-
-def reduce_kernel(axis, n, x_ref, o_ref, parts, total, s1, r1, s2, r2):
-    me = greet(axis, n)
-    copies = [
-        send(axis, n, me, k, x_ref.at[lax.rem(me + k, n)], parts.at[k - 1], (s1, r1))
-        for k in range(1, n)
-    ]
-    acc = x_ref[me]
-    for k in range(1, n):
-        copies[k - 1].wait_recv()
-        acc = acc + parts[k - 1]
-    total[me] = acc
-    back = [send(axis, n, me, k, total.at[me], total.at[me], (s2, r2)) for k in range(1, n)]
-    for copy in copies:
-        copy.wait_send()
-    for copy in back:
-        copy.wait()
-    o_ref[...] = total[...]
-
-
-def reduced(x, axis, ident):
-    n = x.shape[0]
-    vmem = pl.BlockSpec(memory_space=pltpu.VMEM)
-    return pl.pallas_call(
-        functools.partial(reduce_kernel, axis, n),
-        out_shape=jax.ShapeDtypeStruct(x.shape, x.dtype),
-        in_specs=[vmem],
-        out_specs=vmem,
-        scratch_shapes=[
-            pltpu.VMEM((n - 1,) + x.shape[1:], x.dtype),
-            pltpu.VMEM(x.shape, x.dtype),
-        ]
-        + [pltpu.SemaphoreType.DMA((n - 1,))] * 4,
-        compiler_params=pltpu.CompilerParams(collective_id=ident, has_side_effects=True),
-    )(x)
-
-
-def split(x, n):
-    rows, length = x.shape
-    return x.reshape(rows, n, length // n).transpose(1, 0, 2)
-
-
-def join(x):
-    n, rows, part = x.shape
-    return x.transpose(1, 0, 2).reshape(rows, n * part)
-
-
-def all_reduced(x, axis, ident):
-    return join(reduced(split(x, lax.axis_size(axis)), axis, ident))
 
 
 def nt(left, right, **how):
@@ -137,26 +63,26 @@
     )
 
 
-def scatters(n, me, part, got, sems):
+def scatters(axis, n, me, part, got, sems):
     per = part.shape[0] // n
     return [
         copy_to(
-            "fsdp", n, me, k, part.at[pl.ds(lax.rem(me + k, n) * per, per)], got.at[k - 1], sems
+            axis, n, me, k, part.at[pl.ds(lax.rem(me + k, n) * per, per)], got.at[k - 1], sems
         )
         for k in range(1, n)
     ]
 
 
-def gathers(n, me, total, sems):
+def gathers(axis, n, me, total, sems):
     per = total.shape[0] // n
     own = total.at[pl.ds(me * per, per)]
-    return [copy_to("fsdp", n, me, k, own, own, sems) for k in range(1, n)]
-
-
-def summed(n, me, part, got, total, sems):
+    return [copy_to(axis, n, me, k, own, own, sems) for k in range(1, n)]
+
+
+def summed(axis, n, me, part, got, total, sems):
     per = part.shape[0] // n
     acc = part[pl.ds(me * per, per)]
-    for k, copy in enumerate(scatters(n, me, part, got, sems)):
+    for k, copy in enumerate(scatters(axis, n, me, part, got, sems)):
         copy.wait()
         acc = acc + got[k]
     total[pl.ds(me * per, per)] = acc
@@ -164,11 +90,12 @@
 
 def main_kernel(
     nstate, factor, nblocks, nf, nc,
-    inner, upstream, weight, reach_ref, rates, scale,
-    coef_out, grad_out, carried_ref,
+    inner, upstream, weight, reach_ref, rates, scale, skip,
+    out, proj_out,
     base, inverse, scaled_all, weighted_all, cross, part, got, coef, gpart, ggot, grad,
     states, before, terms, pack, packed, arriving, leaving, home, arrived, adjoint,
-    s1, r1, s2, r2, s3, r3, s4, r4, s5, r5, s6, r6,
+    carried_ref, proj, ppart, pgot, ptotal,
+    s1, r1, s2, r2, s3, r3, s4, r4, s5, r5, s6, r6, s7, r7, s8, r8,
 ):
     step = pl.program_id(0)
     size = 2 * nstate
@@ -198,16 +125,16 @@
     @pl.when(step == nblocks)
     def _():
         pl.semaphore_wait(barrier, nf + nc - 2)
-        for copy in scatters(nf, f, part, got, (s1, r1)):
+        for copy in scatters("fsdp", nf, f, part, got, (s1, r1)):
             copy.start()
 
     @pl.when(step == nblocks + nblocks // 2)
     def _():
-        summed(nf, f, part, got, coef, (s1, r1))
-        for copy in gathers(nf, f, coef, (s2, r2)):
-            copy.start()
-
-    @pl.when(step >= nblocks)
+        summed("fsdp", nf, f, part, got, coef, (s1, r1))
+        for copy in gathers("fsdp", nf, f, coef, (s2, r2)):
+            copy.start()
+
+    @pl.when((step >= nblocks) & (step < 2 * nblocks))
     def _():
         j = step - nblocks
         total = jnp.zeros((BLK, BLK), jnp.float32)
@@ -219,7 +146,7 @@
 
     @pl.when(step == 2 * nblocks - 1)
     def _():
-        for copy in gathers(nf, f, coef, (s2, r2)):
+        for copy in gathers("fsdp", nf, f, coef, (s2, r2)):
             copy.wait()
 
         def local_states(j, carry):
@@ -291,49 +218,66 @@
             return carry
 
         lax.fori_loop(0, nblocks, local_grads, 0)
-        for copy in scatters(nf, f, gpart, ggot, (s5, r5)):
-            copy.start()
-        coef_out[...] = coef[...]
-        summed(nf, f, gpart, ggot, grad, (s5, r5))
-        final = gathers(nf, f, grad, (s6, r6))
+        for copy in scatters("fsdp", nf, f, gpart, ggot, (s5, r5)):
+            copy.start()
+        proj[...] = jnp.zeros_like(proj)
+        summed("fsdp", nf, f, gpart, ggot, grad, (s5, r5))
+        final = gathers("fsdp", nf, f, grad, (s6, r6))
         for copy in final:
             copy.start()
         for copy in final:
             copy.wait()
-        grad_out[...] = grad[...]
-
-
-def final_kernel(
-    nstate, factor, inner, upstream, coef, reach_ref, rates, scale,
-    carried, grad, weight, skip, out, proj, base, inverse,
-):
-    @pl.when(pl.program_id(0) == 0)
-    def _():
-        fill(rates, scale, base, inverse)
-        proj[...] = jnp.zeros_like(proj)
-
-    reach = reach_ref[...]
-    short = coef[0].astype(jnp.bfloat16)
-    write, read = short[:nstate], short[nstate:]
-    row = lax.broadcasted_iota(jnp.int32, (BLK, BLK), 0)
-    col = lax.broadcasted_iota(jnp.int32, (BLK, BLK), 1)
-    turned = jnp.where(col >= row, tn(write, read), 0.0).astype(jnp.bfloat16)
-    full = grad[0]
-    high = full.astype(jnp.bfloat16)
-    rest = full - high.astype(jnp.float32)
-    middle = rest.astype(jnp.bfloat16)
-    low = (rest - middle.astype(jnp.float32)).astype(jnp.bfloat16)
-    stack = jnp.concatenate([high, middle, low], axis=0)
-    size = 2 * nstate
-    for cols in pieces(inner.shape[1]):
-        weighted = weighted_of(upstream, base, reach, cols)
-        mixed = factor * nn(turned, weighted) + tn(write, carried[0, :, cols])
-        value = inverse[:, cols] * (1.0 / reach) * mixed
-        value = value + skip[:, cols] * upstream[:, cols].astype(jnp.float32)
-        value = value + tn(high, weight[:, cols])
-        out[:, cols] = value.astype(jnp.bfloat16)
-        three = nn(stack, inner[:, cols])
-        proj[:, cols] = proj[:, cols] + (three[:size] + (three[size : 2 * size] + three[2 * size :]))
+
+    @pl.when((step >= 2 * nblocks) & (step < 3 * nblocks))
+    def _():
+        full = grad[step - 2 * nblocks]
+        high = full.astype(jnp.bfloat16)
+        rest = full - high.astype(jnp.float32)
+        middle = rest.astype(jnp.bfloat16)
+        low = (rest - middle.astype(jnp.float32)).astype(jnp.bfloat16)
+        stack = jnp.concatenate([high, middle, low], axis=0)
+        for cols in pieces(channels):
+            three = nn(stack, inner[:, cols])
+            proj[:, cols] = proj[:, cols] + (
+                three[:size] + (three[size : 2 * size] + three[2 * size :])
+            )
+
+    @pl.when(step == 3 * nblocks)
+    def _():
+        for d in range(nc):
+            ppart[d] = proj[:, d * width : (d + 1) * width]
+        for copy in scatters("ctx", nc, c, ppart, pgot, (s7, r7)):
+            copy.start()
+
+    @pl.when(step == 3 * nblocks + (5 * nblocks) // 8)
+    def _():
+        summed("ctx", nc, c, ppart, pgot, ptotal, (s7, r7))
+        for copy in gathers("ctx", nc, c, ptotal, (s8, r8)):
+            copy.start()
+
+    @pl.when(step >= 3 * nblocks)
+    def _():
+        j = step - 3 * nblocks
+        short = coef[j].astype(jnp.bfloat16)
+        write, read = short[:nstate], short[nstate:]
+        row = lax.broadcasted_iota(jnp.int32, (BLK, BLK), 0)
+        col = lax.broadcasted_iota(jnp.int32, (BLK, BLK), 1)
+        turned = jnp.where(col >= row, tn(write, read), 0.0).astype(jnp.bfloat16)
+        high = grad[j].astype(jnp.bfloat16)
+        recip = 1.0 / reach_ref[j]
+        for cols in pieces(channels):
+            mixed = factor * nn(turned, weighted_all[j, :, cols]) + tn(write, carried_ref[j, :, cols])
+            value = inverse[:, cols] * recip * mixed
+            value = value + skip[:, cols] * upstream[:, cols].astype(jnp.float32)
+            value = value + tn(high, weight[:, cols])
+            out[:, cols] = value.astype(jnp.bfloat16)
+
+    @pl.when(step == 4 * nblocks - 1)
+    def _():
+        for copy in gathers("ctx", nc, c, ptotal, (s8, r8)):
+            copy.wait()
+        for d in range(nc):
+            proj_out[:, d * width : (d + 1) * width] = ptotal[d] / (nblocks * BLK * nc)
 
 
 def local(inner, proj_weight, rates, keep, skip, upstream):
@@ -346,10 +290,6 @@
     scale = jnp.sqrt(-jnp.expm1(-2.0 * rates))[None]
     rates = rates[None]
     reach = jnp.cumprod(keep.reshape(nblocks, BLK), axis=1).reshape(length, 1)
-    params = pltpu.CompilerParams(
-        dimension_semantics=("arbitrary",), vmem_limit_bytes=48 * 2**20
-    )
-
     nf, nc = lax.axis_size("fsdp"), lax.axis_size("ctx")
     bf16 = jnp.bfloat16
     whole = pl.BlockSpec(memory_space=pltpu.VMEM)
@@ -369,20 +309,36 @@
         + [pltpu.VMEM((nc, size + 8, width), f32)] * 2
         + [pltpu.VMEM((nc, size, width), f32)] * 2
         + [pltpu.VMEM((size, channels), f32), pltpu.VMEM((nstate, channels), f32)]
+        + [pltpu.VMEM(entry, bf16), pltpu.VMEM((size, channels), f32)]
+        + [pltpu.VMEM((nc, size, width), f32)]
+        + [pltpu.VMEM((nc - 1, 1, size, width), f32), pltpu.VMEM((nc, size, width), f32)]
         + [pltpu.SemaphoreType.DMA((nf - 1,))] * 4
         + [pltpu.SemaphoreType.DMA((nc - 1,))] * 4
         + [pltpu.SemaphoreType.DMA((nf - 1,))] * 4
-    )
-    coef, grad, carried = pl.pallas_call(
+        + [pltpu.SemaphoreType.DMA((nc - 1,))] * 4
+    )
+    last = nblocks - 1
+
+    def inner_at(i):
+        return (jnp.where(i < 2 * nblocks, jnp.minimum(i, last), jnp.minimum(i - 2 * nblocks, last)), 0)
+
+    def upstream_at(i):
+        first = jnp.clip(i - nblocks, 0, last)
+        return (jnp.where(i < 2 * nblocks, first, jnp.maximum(i - 3 * nblocks, 0)), 0)
+
+    return pl.pallas_call(
         functools.partial(main_kernel, nstate, factor, nblocks, nf, nc),
-        grid=(2 * nblocks,),
+        grid=(4 * nblocks,),
         in_specs=[
-            pl.BlockSpec((BLK, channels), lambda i: (jnp.minimum(i, nblocks - 1), 0)),
-            pl.BlockSpec((BLK, channels), lambda i: (jnp.maximum(i - nblocks, 0), 0)),
-            whole, whole, whole, whole,
+            pl.BlockSpec((BLK, channels), inner_at),
+            pl.BlockSpec((BLK, channels), upstream_at),
+            whole, whole, whole, whole, whole,
         ],
-        out_specs=[whole, whole, whole],
-        out_shape=[shape(coefs, f32), shape(coefs, f32), shape(entry, bf16)],
+        out_specs=[
+            pl.BlockSpec((BLK, channels), lambda i: (jnp.maximum(i - 3 * nblocks, 0), 0)),
+            whole,
+        ],
+        out_shape=[shape((length, channels), bf16), shape((size, channels), f32)],
         scratch_shapes=scratch,
         compiler_params=pltpu.CompilerParams(
             dimension_semantics=("arbitrary",),
@@ -390,26 +346,9 @@
             collective_id=0,
             has_side_effects=True,
         ),
-    )(inner, upstream, proj_weight, reach.reshape(nblocks, BLK, 1), rates, scale)
-
-    tokens = pl.BlockSpec((BLK, channels), lambda i: (i, 0))
-    column = pl.BlockSpec((BLK, 1), lambda i: (i, 0))
-    line = pl.BlockSpec((1, channels), lambda i: (0, 0))
-    fixed = pl.BlockSpec((size, channels), lambda i: (0, 0))
-    block_coef = pl.BlockSpec((1, size, BLK), lambda i: (i, 0, 0))
-    block_state = pl.BlockSpec((1, nstate, channels), lambda i: (i, 0, 0))
-    input_grad, proj = pl.pallas_call(
-        functools.partial(final_kernel, nstate, factor),
-        grid=(nblocks,),
-        in_specs=[tokens, tokens, block_coef, column, line, line]
-        + [block_state, block_coef, fixed, line],
-        out_specs=[tokens, fixed],
-        out_shape=[shape((length, channels), bf16), shape((size, channels), f32)],
-        scratch_shapes=tables,
-        compiler_params=params,
-    )(inner, upstream, coef, reach, rates, scale, carried, grad, proj_weight, skip[None])
-    total = all_reduced(proj, "ctx", 1)
-    return (input_grad, total / (length * nc))
+    )(
+        inner, upstream, proj_weight, reach.reshape(nblocks, BLK, 1), rates, scale, skip[None]
+    )
 
 
 def solution(mesh):

time: 102 us -> 93.4 us (0.916)
  Pallas kernels: 90 us -> 78.5 us
  local copies, waits for them, and re-layouts: 6.98 us -> 11.4 us
  other arithmetic: 3.04 us -> 2 us
    pallas_call x2 -> x0, Pallas kernels: 29.9 us -> none  [the longest x1 16.7 us: local(): pl.pallas_call(functools.partial(final_kernel, nstate, factor), grid=(nbl...]
    pallas_call x1, Pallas kernels: 60.1 us -> 78.5 us  [local(): pl.pallas_call(functools.partial(main_kernel, nstate, factor, nblocks, nf...]
    unnamed x14 -> x4, local copies, waits for them, and re-layouts: 2.95 us -> 9.19 us
where the time goes in v4:
time: 93.4 us; the launch traced here: 92.6 us
  Pallas kernels  78.5 us (84%)
  local copies, waits for them, and re-layouts  11.4 us (12%)
  other arithmetic  2 us (2%)
    pallas_call x1, Pallas kernels, local(): pl.pallas_call(functools.partial(main_kernel, nstate, factor, nblocks, nf...  78.5 us
    unnamed x4, local copies, waits for them, and re-layouts  9.19 us

profile of v4, /device:TPU:0, one launch (start us, length us, event | category | flops | bytes accessed | tf_op | source)
XLA Modules:
  0.0 92.6 jit_solution(7299203721417144977)
XLA Ops:
  0.6 0.7 copy.9
  1.3 0.6 reduce-window.6
  1.9 0.2 slice_reduce_fusion
  2.1 0.1 multiply_bitcast_fusion
  2.2 1.3 %negate_sqrt_fusion = f32[2048]{0:T(1024)} fusion(f32[2048]{0:T(1024)} %param.8), kind=kLoop, calls=%fused_computation.1 | loop fusion | flops 4096 | bytes 16384 | tf_op jit(solution)/shard_map/sqrt | solution.py:290
  3.5 1.3 %copy.10.reach_ref = f32[8,256,1]{2,1,0:T(8,128)} copy(f32[8,256,1]{1,0,2:T(8,128)S(1)} %multiply_bitcast_fusion) | data formatting | bytes 16384 | tf_op jit(solution)/shard_map/mul
  4.8 78.5 %shard_map.77 = (bf16[2048,2048]{1,0:T(8,128)(2,1)}, f32[32,2048]{1,0:T(8,128)}) custom-call(bf16[2048,2048]{1,0:T(8,128)(2,1)} %inner.1, bf16[2048,2048]{1,0:T(8,128)(2,1)} %upstream.1, bf16[32,2048]{1,0:T(8,128)(2,1)} %weight.1, f32[8,256,1]{2,1,0:T(8,128)} %copy.10.reach_ref, f32[1,2048]{1,0:T(1,128)} %bitcast.6, f32[1,2048]{1,0:T(1,128)} %bitcast.7, ...), custom_call_target="tpu_custom_call" | custom-call | tf_op jit(solution)/shard_map/pallas_call | solution.py:329
  83.4 0.0 copy-start
  83.4 8.5 %copy.13 = bf16[2048,2048]{1,0:T(8,128)(2,1)} copy(bf16[2048,2048]{1,0:T(8,128)(2,1)} %get-tuple-element.4) | data formatting | bytes 16777216
  91.9 0.0 copy-done
  91.9 0.7 copy.14
  (2 shorter events, 0.0 us)
Async XLA Ops:
  83.4 8.5 %copy-start = (f32[32,2048]{1,0:T(8,128)S(1)}, f32[32,2048]{1,0:T(8,128)}, u32[]{:S(2)}) copy-start(f32[32,2048]{1,0:T(8,128)} %get-tuple-element.5) | copy-start | bytes 786436

commit v5 on v4

--- a/solution.py
+++ b/solution.py
@@ -71,6 +71,19 @@
         )
         for k in range(1, n)
     ]
+
+
+def slice_to(n, me, owner, part, got, sems):
+    per = part.shape[0] // n
+    k = lax.rem(owner - me + n, n)
+    return pltpu.make_async_remote_copy(
+        src_ref=part.at[pl.ds(owner * per, per)],
+        dst_ref=got.at[k - 1],
+        send_sem=sems[0].at[k - 1],
+        recv_sem=sems[1].at[k - 1],
+        device_id={"fsdp": owner},
+        device_id_type=MESH,
+    )
 
 
 def gathers(axis, n, me, total, sems):
@@ -122,13 +135,15 @@
         for cols in pieces(channels):
             scaled_all[step, :, cols] = scaled_of(inner, inverse, reach_ref[step], cols)
 
-    @pl.when(step == nblocks)
+    @pl.when(step == nblocks - nf)
     def _():
         pl.semaphore_wait(barrier, nf + nc - 2)
-        for copy in scatters("fsdp", nf, f, part, got, (s1, r1)):
-            copy.start()
-
-    @pl.when(step == nblocks + nblocks // 2)
+
+    @pl.when((step >= nblocks - nf) & (step < nblocks) & (step - (nblocks - nf) != f))
+    def _():
+        slice_to(nf, f, step - (nblocks - nf), part, got, (s1, r1)).start()
+
+    @pl.when(step == nblocks + (3 * nblocks) // 8)
     def _():
         summed("fsdp", nf, f, part, got, coef, (s1, r1))
         for copy in gathers("fsdp", nf, f, coef, (s2, r2)):
@@ -175,6 +190,15 @@
         for copy in out:
             copy.start()
         arriving[c] = packed[c]
+        exact = dict(precision=lax.Precision.HIGHEST)
+
+        def local_products(j, carry):
+            wide = coef[j]
+            gpart[j, :nstate] = factor * nn(wide[nstate:], cross[j], **exact)
+            gpart[j, nstate:] = factor * nt(wide[:nstate], cross[j], **exact)
+            return carry
+
+        lax.fori_loop(0, nblocks, local_products, 0)
         for copy in out:
             copy.wait()
         state = jnp.zeros((nstate, width), jnp.float32)
@@ -197,10 +221,9 @@
         for d in range(nc):
             arrived[:, d * width : (d + 1) * width] = home[d]
         adjoint[...] = arrived[nstate:]
-        exact = dict(precision=lax.Precision.HIGHEST)
-
-        def local_grads(k, carry):
-            j = nblocks - 1 - k
+
+        def local_grads(k, last):
+            j = last - k
             write_part = jnp.zeros((nstate, BLK), jnp.float32)
             read_part = jnp.zeros((nstate, BLK), jnp.float32)
             for cols in pieces(channels):
@@ -212,14 +235,18 @@
                 state = states[j, :, cols] + before[j, :, cols] * arrived[:nstate, cols]
                 write_part = write_part + nt(carried, scaled_all[j, :, cols])
                 read_part = read_part + nt(state.astype(jnp.bfloat16), weighted_all[j, :, cols])
-            wide = coef[j]
-            gpart[j, :nstate] = factor * nn(wide[nstate:], cross[j], **exact) + write_part
-            gpart[j, nstate:] = factor * (read_part + nt(wide[:nstate], cross[j], **exact))
-            return carry
-
-        lax.fori_loop(0, nblocks, local_grads, 0)
-        for copy in scatters("fsdp", nf, f, gpart, ggot, (s5, r5)):
-            copy.start()
+            gpart[j, :nstate] = gpart[j, :nstate] + write_part
+            gpart[j, nstate:] = gpart[j, nstate:] + factor * read_part
+            return last
+
+        per = nblocks // nf
+        for owner in reversed(range(nf)):
+            lax.fori_loop(0, per, local_grads, (owner + 1) * per - 1)
+
+            @pl.when(f != owner)
+            def _(owner=owner):
+                slice_to(nf, f, owner, gpart, ggot, (s5, r5)).start()
+
         proj[...] = jnp.zeros_like(proj)
         summed("fsdp", nf, f, gpart, ggot, grad, (s5, r5))
         final = gathers("fsdp", nf, f, grad, (s6, r6))
@@ -278,6 +305,10 @@
             copy.wait()
         for d in range(nc):
             proj_out[:, d * width : (d + 1) * width] = ptotal[d] / (nblocks * BLK * nc)
+
+
+def place_kernel(source, target):
+    target[...] = source[...]
 
 
 def local(inner, proj_weight, rates, keep, skip, upstream):
@@ -326,7 +357,7 @@
         first = jnp.clip(i - nblocks, 0, last)
         return (jnp.where(i < 2 * nblocks, first, jnp.maximum(i - 3 * nblocks, 0)), 0)
 
-    return pl.pallas_call(
+    input_grad, proj_grad = pl.pallas_call(
         functools.partial(main_kernel, nstate, factor, nblocks, nf, nc),
         grid=(4 * nblocks,),
         in_specs=[
@@ -349,6 +380,16 @@
     )(
         inner, upstream, proj_weight, reach.reshape(nblocks, BLK, 1), rates, scale, skip[None]
     )
+    rows = pl.BlockSpec((BLK, channels), lambda i: (i, 0))
+    placed = pl.pallas_call(
+        place_kernel,
+        grid=(nblocks,),
+        in_specs=[rows],
+        out_specs=rows,
+        out_shape=shape((length, channels), bf16),
+        compiler_params=pltpu.CompilerParams(dimension_semantics=("arbitrary",)),
+    )(input_grad)
+    return (placed, proj_grad)
 
 
 def solution(mesh):

time: 93.4 us -> 92.9 us (level)
  local copies, waits for them, and re-layouts: 11.4 us -> 2.91 us
  Pallas kernels: 78.5 us -> 86.3 us
    pallas_call x0 -> x1, Pallas kernels: none -> 9 us  [local(): pl.pallas_call(place_kernel, grid=(nblocks,), in_specs=[rows], out_specs=...]
    unnamed x4 -> x3, local copies, waits for them, and re-layouts: 9.19 us -> 0.71 us
    pallas_call x1, Pallas kernels: 78.5 us -> 77.3 us  [local(): pl.pallas_call(functools.partial(main_kernel, nstate, factor, nblocks, nf...]
where the time goes in v5:
time: 92.9 us; the launch traced here: 91.9 us
  Pallas kernels  86.3 us (93%)
  local copies, waits for them, and re-layouts  2.91 us (3%)
  other arithmetic  2 us (2%)
    pallas_call x1, Pallas kernels, local(): pl.pallas_call(functools.partial(main_kernel, nstate, factor, nblocks, nf...  77.3 us
    pallas_call x1, Pallas kernels, local(): pl.pallas_call(place_kernel, grid=(nblocks,), in_specs=[rows], out_specs=...  9 us

profile of v5, /device:TPU:0, one launch (start us, length us, event | category | flops | bytes accessed | tf_op | source)
XLA Modules:
  0.0 91.9 jit_solution(3568974524320903763)
XLA Ops:
  0.6 0.7 copy.9
  1.3 0.6 reduce-window.6
  1.9 0.2 slice_reduce_fusion
  2.1 0.1 multiply_bitcast_fusion
  2.2 1.3 %negate_sqrt_fusion = f32[2048]{0:T(1024)} fusion(f32[2048]{0:T(1024)} %param.8), kind=kLoop, calls=%fused_computation.1 | loop fusion | flops 4096 | bytes 16384 | tf_op jit(solution)/shard_map/sqrt | solution.py:321
  3.5 1.3 %copy.10.reach_ref = f32[8,256,1]{2,1,0:T(8,128)} copy(f32[8,256,1]{1,0,2:T(8,128)S(1)} %multiply_bitcast_fusion) | data formatting | bytes 16384 | tf_op jit(solution)/shard_map/mul
  4.8 77.3 %shard_map.77 = (bf16[2048,2048]{1,0:T(8,128)(2,1)}, f32[32,2048]{1,0:T(8,128)}) custom-call(bf16[2048,2048]{1,0:T(8,128)(2,1)} %inner.1, bf16[2048,2048]{1,0:T(8,128)(2,1)} %upstream.1, bf16[32,2048]{1,0:T(8,128)(2,1)} %weight.1, f32[8,256,1]{2,1,0:T(8,128)} %copy.10.reach_ref, f32[1,2048]{1,0:T(1,128)} %bitcast.6, f32[1,2048]{1,0:T(1,128)} %bitcast.7, ...), custom_call_target="tpu_custom_call" | custom-call | tf_op jit(solution)/shard_map/pallas_call | solution.py:360
  82.2 0.0 copy-start
  82.2 9.0 %shard_map.78 = bf16[2048,2048]{1,0:T(8,128)(2,1)} custom-call(bf16[2048,2048]{1,0:T(8,128)(2,1)} %get-tuple-element.4.source), custom_call_target="tpu_custom_call" | custom-call | tf_op jit(solution)/shard_map/pallas_call | solution.py:384
  91.2 0.0 copy-done
  91.2 0.7 copy.12
  (2 shorter events, 0.0 us)
Async XLA Ops:
  82.2 9.0 %copy-start = (f32[32,2048]{1,0:T(8,128)S(1)}, f32[32,2048]{1,0:T(8,128)}, u32[]{:S(2)}) copy-start(f32[32,2048]{1,0:T(8,128)} %get-tuple-element.9) | copy-start | bytes 786436

commit v6 on v5

--- a/solution.py
+++ b/solution.py
@@ -297,7 +297,7 @@
             value = inverse[:, cols] * recip * mixed
             value = value + skip[:, cols] * upstream[:, cols].astype(jnp.float32)
             value = value + tn(high, weight[:, cols])
-            out[:, cols] = value.astype(jnp.bfloat16)
+            out[pl.ds(j * BLK, BLK), cols] = value.astype(jnp.bfloat16)
 
     @pl.when(step == 4 * nblocks - 1)
     def _():
@@ -308,7 +308,7 @@
 
 
 def place_kernel(source, target):
-    target[...] = source[...]
+    target[...] = source[pl.ds(pl.program_id(0) * BLK, BLK), :]
 
 
 def local(inner, proj_weight, rates, keep, skip, upstream):
@@ -366,14 +366,14 @@
             whole, whole, whole, whole, whole,
         ],
         out_specs=[
-            pl.BlockSpec((BLK, channels), lambda i: (jnp.maximum(i - 3 * nblocks, 0), 0)),
+            whole,
             whole,
         ],
-        out_shape=[shape((length, channels), bf16), shape((size, channels), f32)],
+        out_shape=[pltpu.VMEM((length, channels), bf16), shape((size, channels), f32)],
         scratch_shapes=scratch,
         compiler_params=pltpu.CompilerParams(
             dimension_semantics=("arbitrary",),
-            vmem_limit_bytes=56 * 2**20,
+            vmem_limit_bytes=46 * 2**20,
             collective_id=0,
             has_side_effects=True,
         ),
@@ -384,10 +384,12 @@
     placed = pl.pallas_call(
         place_kernel,
         grid=(nblocks,),
-        in_specs=[rows],
+        in_specs=[whole],
         out_specs=rows,
         out_shape=shape((length, channels), bf16),
-        compiler_params=pltpu.CompilerParams(dimension_semantics=("arbitrary",)),
+        compiler_params=pltpu.CompilerParams(
+            dimension_semantics=("arbitrary",), vmem_limit_bytes=32 * 2**20
+        ),
     )(input_grad)
     return (placed, proj_grad)
 

time: 92.9 us -> 87 us (0.936)
  Pallas kernels: 86.3 us -> 80.9 us
    pallas_call x1, Pallas kernels: 9 us -> 4.52 us  [local(): pl.pallas_call(place_kernel, grid=(nblocks,), in_specs=[whole], out_specs...]
    pallas_call x1, Pallas kernels: 77.3 us -> 76.4 us  [local(): pl.pallas_call(functools.partial(main_kernel, nstate, factor, nblocks, nf...]
where the time goes in v6:
time: 87 us; the launch traced here: 86.5 us
  Pallas kernels  80.9 us (93%)
  local copies, waits for them, and re-layouts  2.91 us (3%)
  other arithmetic  2 us (2%)
    pallas_call x1, Pallas kernels, local(): pl.pallas_call(functools.partial(main_kernel, nstate, factor, nblocks, nf...  76.4 us
    pallas_call x1, Pallas kernels, local(): pl.pallas_call(place_kernel, grid=(nblocks,), in_specs=[whole], out_specs...  4.52 us

profile of v6, /device:TPU:0, one launch (start us, length us, event | category | flops | bytes accessed | tf_op | source)
XLA Modules:
  0.0 86.5 jit_solution(5320690613521218460)
XLA Ops:
  0.6 0.7 copy.9
  1.3 0.6 reduce-window.6
  1.9 0.2 slice_reduce_fusion
  2.1 0.1 multiply_bitcast_fusion
  2.2 1.3 %negate_sqrt_fusion = f32[2048]{0:T(1024)} fusion(f32[2048]{0:T(1024)} %param.8), kind=kLoop, calls=%fused_computation.1 | loop fusion | flops 4096 | bytes 16384 | tf_op jit(solution)/shard_map/sqrt | solution.py:321
  3.5 1.3 %copy.10.reach_ref = f32[8,256,1]{2,1,0:T(8,128)} copy(f32[8,256,1]{1,0,2:T(8,128)S(1)} %multiply_bitcast_fusion) | data formatting | bytes 16384 | tf_op jit(solution)/shard_map/mul
  4.8 76.4 %shard_map.77 = (bf16[2048,2048]{1,0:T(8,128)(2,1)S(1)}, f32[32,2048]{1,0:T(8,128)}) custom-call(bf16[2048,2048]{1,0:T(8,128)(2,1)} %inner.1, bf16[2048,2048]{1,0:T(8,128)(2,1)} %upstream.1, bf16[32,2048]{1,0:T(8,128)(2,1)} %weight.1, f32[8,256,1]{2,1,0:T(8,128)} %copy.10.reach_ref, f32[1,2048]{1,0:T(1,128)} %bitcast.6, f32[1,2048]{1,0:T(1,128)} %bitcast.7, ...), custom_call_target="tpu_custom_call" | custom-call | tf_op jit(solution)/shard_map/pallas_call | solution.py:360
  81.3 0.0 copy-start
  81.3 4.5 %shard_map.78 = bf16[2048,2048]{1,0:T(8,128)(2,1)} custom-call(bf16[2048,2048]{1,0:T(8,128)(2,1)S(1)} %get-tuple-element.4.source), custom_call_target="tpu_custom_call" | custom-call | tf_op jit(solution)/shard_map/pallas_call | solution.py:384
  85.8 0.0 copy-done
  85.8 0.7 copy.12
  (2 shorter events, 0.0 us)
Async XLA Ops:
  81.3 4.5 %copy-start = (f32[32,2048]{1,0:T(8,128)S(1)}, f32[32,2048]{1,0:T(8,128)}, u32[]{:S(2)}) copy-start(f32[32,2048]{1,0:T(8,128)} %get-tuple-element.9) | copy-start | bytes 786436
